TPU v7x, 512 devices: a whole 4x4x16 slice. The times are simulated.
512 devices in a mesh: gx: 32 (over z, core), gy: 16 (over y, x).
Axes of the slice: x: 4, y: 4, z: 16, core: 2. Of those that a mesh axis runs over, the one named last changes fastest.
Arguments:
- density: float32 [2, 512, 512, 128], P(None, 'gx', 'gy'), may hold values from 0.2 to 1
- cotangent: float32 [2, 512, 512, 128], P(None, 'gx', 'gy'), may hold values from -6 to 6
- adhesion: float32 [2, 2], replicated, may hold values from 1 to 3
Outputs:
- density_bar: float32 [2, 512, 512, 128], P(None, 'gx', 'gy')
All inputs are finite; a program needn't handle non-finite values.
Results may differ from a plain program's by a relative error of at most 0.000084.
Values sent between devices are 32-bit elements; how exact they have to be, the bound alone decides.
No kernel may reach another device: no remote copies, remote signals or barrier semaphores. Data moves between devices by JAX's collectives and lax.ppermute only.
A program may use at most 64 MiB of HBM per device.

v0:
```python
import jax
import jax.numpy as jnp
from jax import lax
from jax.sharding import PartitionSpec as P

RADIUS = 16


time_step = 0.5
smoothing = 0.1
highest = lax.Precision.HIGHEST


def padded(cells, sides, width):
    for axis, dim in sides:
        count = lax.axis_size(axis)
        ends = count - 1
        head = lax.slice_in_dim(cells, 0, width, axis=dim)
        tail = lax.slice_in_dim(cells, cells.shape[dim] - width, cells.shape[dim], axis=dim)
        cells = jnp.concatenate(
            [
                lax.ppermute(tail, axis, [(i, (i + 1) % count) for i in range(ends)]),
                cells,
                lax.ppermute(head, axis, [((i + 1) % count, i) for i in range(ends)]),
            ],
            axis=dim,
        )
    return cells


def kernel_weight(offsets, antisym):
    magnitude = jnp.abs(offsets)
    weights = jnp.where(magnitude <= RADIUS, 1.0 - magnitude / (RADIUS + 1.0), 0.0)
    if antisym:
        weights = weights * offsets / RADIUS
    return weights


def kernel_norm(antisym):
    offsets = jnp.arange(-RADIUS, RADIUS + 1).astype(jnp.float32)
    weights = kernel_weight(offsets, antisym)
    return jnp.sqrt(jnp.sum(weights * weights))


def band_matrix(outputs, inputs, lead_in, antisym):
    row_index = lax.broadcasted_iota(jnp.int32, (outputs, inputs), 0)
    col_index = lax.broadcasted_iota(jnp.int32, (outputs, inputs), 1)
    offsets = (col_index - row_index - lead_in).astype(jnp.float32)
    return kernel_weight(offsets, antisym) / kernel_norm(antisym)


def along_x(matrix, values):
    return jnp.einsum("ck,fkyz->fcyz", matrix, values, precision=highest)


def along_y(matrix, values):
    return jnp.einsum("ck,fxkz->fxcz", matrix, values, precision=highest)


def along_z(matrix, values):
    return jnp.einsum("ck,fxyk->fxyc", matrix, values, precision=highest)


def face_terms(
    lower_density, upper_density, lower_cot, upper_cot, lower_velocity, upper_velocity, valid
):
    face_velocity = 0.5 * (lower_velocity + upper_velocity)
    magnitude = jnp.sqrt(face_velocity * face_velocity + smoothing * smoothing)
    flux_bar = jnp.where(valid, time_step * (upper_cot - lower_cot), 0.0)
    to_lower = flux_bar * 0.5 * (face_velocity + magnitude)
    to_upper = flux_bar * 0.5 * (face_velocity - magnitude)
    velocity_bar = flux_bar * (
        0.5 * (lower_density + upper_density)
        - 0.5 * face_velocity / magnitude * (upper_density - lower_density)
    )
    return (to_lower, to_upper, velocity_bar)


def raise_z(values):
    return jnp.concatenate([values[..., 1:], jnp.zeros_like(values[..., :1])], 3)


def drop_z(values):
    return jnp.concatenate([jnp.zeros_like(values[..., :1]), values[..., :-1]], 3)


def mix_fields(adhesion, fields):
    return (
        adhesion[:, 0, None, None, None] * fields[0][None]
        + adhesion[:, 1, None, None, None] * fields[1][None]
    )


def send_rims(density, cotangent, velocity_x, velocity_y):
    return padded(
        jnp.concatenate([density, cotangent, velocity_x, velocity_y], 0), (("gx", 1), ("gy", 2)), 1
    )


def body(density, cotangent, adhesion):
    cells_x = density.shape[1]
    cells_y = density.shape[2]
    cells_z = density.shape[3]
    wide_x = cells_x + 2 * RADIUS
    wide_y = cells_y + 2 * RADIUS
    even_x = band_matrix(cells_x, wide_x, RADIUS, False)
    odd_x = band_matrix(cells_x, wide_x, RADIUS, True)
    even_y = band_matrix(cells_y, wide_y, RADIUS, False)
    odd_y = band_matrix(cells_y, wide_y, RADIUS, True)
    even_z = band_matrix(cells_z, cells_z, 0, False)
    odd_z = band_matrix(cells_z, cells_z, 0, True)
    potential = mix_fields(adhesion, density)
    even_in_z = along_z(even_z, potential)
    odd_in_z = along_z(odd_z, potential)
    widened = padded(jnp.concatenate([even_in_z, odd_in_z], 0), (("gy", 2),), RADIUS)
    stacked = jnp.concatenate(
        [
            along_y(even_y, widened[0:2]),
            along_y(odd_y, widened[0:2]),
            along_y(even_y, widened[2:4]),
        ],
        0,
    )
    widened_x = padded(stacked, (("gx", 1),), RADIUS)
    velocity_x = along_x(odd_x, widened_x[0:2])
    velocity_y = along_x(even_x, widened_x[2:4])
    velocity_z = along_x(even_x, widened_x[4:6])
    rims = send_rims(density, cotangent, velocity_x, velocity_y)
    first_x = lax.axis_index("gx") * cells_x
    total_x = cells_x * lax.axis_size("gx")
    face_x = first_x - 1 + lax.broadcasted_iota(jnp.int32, (1, cells_x + 1, 1, 1), 1)
    valid_x = (face_x >= 0) & (face_x + 1 < total_x)
    strip_x = rims[:, :, 1 : cells_y + 1]
    lower_x = strip_x[:, 0 : cells_x + 1]
    upper_x = strip_x[:, 1 : cells_x + 2]
    to_lower, to_upper, velocity_bar = face_terms(
        lower_x[0:2], upper_x[0:2], lower_x[2:4], upper_x[2:4], lower_x[4:6], upper_x[4:6], valid_x
    )
    density_bar = to_lower[:, 1:] + to_upper[:, :cells_x]
    velocity_bar_x = 0.5 * (velocity_bar[:, 1:] + velocity_bar[:, :cells_x])
    first_y = lax.axis_index("gy") * cells_y
    total_y = cells_y * lax.axis_size("gy")
    face_y = first_y - 1 + lax.broadcasted_iota(jnp.int32, (1, 1, cells_y + 1, 1), 2)
    valid_y = (face_y >= 0) & (face_y + 1 < total_y)
    strip_y = rims[:, 1 : cells_x + 1]
    lower_y = strip_y[:, :, 0 : cells_y + 1]
    upper_y = strip_y[:, :, 1 : cells_y + 2]
    to_lower, to_upper, velocity_bar = face_terms(
        lower_y[0:2], upper_y[0:2], lower_y[2:4], upper_y[2:4], lower_y[6:8], upper_y[6:8], valid_y
    )
    density_bar = density_bar + to_lower[:, :, 1:] + to_upper[:, :, :cells_y]
    velocity_bar_y = 0.5 * (velocity_bar[:, :, 1:] + velocity_bar[:, :, :cells_y])
    face_z = lax.broadcasted_iota(jnp.int32, (1, 1, 1, cells_z), 3)
    valid_z = face_z + 1 < cells_z
    to_lower, to_upper, velocity_bar = face_terms(
        density,
        raise_z(density),
        cotangent,
        raise_z(cotangent),
        velocity_z,
        raise_z(velocity_z),
        valid_z,
    )
    density_bar = density_bar + to_lower + drop_z(to_upper)
    velocity_bar_z = 0.5 * (velocity_bar + drop_z(velocity_bar))
    spread_x = jnp.concatenate(
        [
            along_x(odd_x.T, velocity_bar_x),
            along_x(even_x.T, velocity_bar_y),
            along_x(even_x.T, velocity_bar_z),
        ],
        0,
    )
    margins_x = jnp.concatenate([spread_x[:, :RADIUS], spread_x[:, cells_x + RADIUS :]], 1)
    returned_x = padded(margins_x, (("gx", 1),), RADIUS)
    owned_x = (
        spread_x[:, RADIUS : cells_x + RADIUS]
        + returned_x[:, :RADIUS]
        + returned_x[:, 3 * RADIUS :]
    )
    spread_y = jnp.concatenate(
        [
            along_y(even_y.T, owned_x[0:2]) + along_y(odd_y.T, owned_x[2:4]),
            along_y(even_y.T, owned_x[4:6]),
        ],
        0,
    )
    margins_y = jnp.concatenate([spread_y[:, :, :RADIUS], spread_y[:, :, cells_y + RADIUS :]], 2)
    returned_y = padded(margins_y, (("gy", 2),), RADIUS)
    owned_y = (
        spread_y[:, :, RADIUS : cells_y + RADIUS]
        + jnp.pad(returned_y[:, :, :RADIUS], ((0, 0), (0, 0), (0, cells_y - RADIUS), (0, 0)))
        + jnp.pad(returned_y[:, :, 3 * RADIUS :], ((0, 0), (0, 0), (cells_y - RADIUS, 0), (0, 0)))
    )
    potential_bar = along_z(even_z.T, owned_y[0:2]) + along_z(odd_z.T, owned_y[2:4])
    return (
        cotangent
        + density_bar
        + adhesion[0, :, None, None, None] * potential_bar[0][None]
        + adhesion[1, :, None, None, None] * potential_bar[1][None]
    )


def solution(mesh):
    return jax.shard_map(
        body,
        mesh=mesh,
        in_specs=(P(None, "gx", "gy", None), P(None, "gx", "gy", None), P()),
        out_specs=P(None, "gx", "gy", None),
        check_vma=False,
    )
```

profile of v0, /device:TPU:103, one launch (start us, length us, event | category | flops | bytes accessed | tf_op | source)
XLA Modules:
  0.0 144.7 jit_solution(14138783565205195664)
XLA Ops:
  0.0 0.6 multiply_reduce_fusion.1
  0.6 0.6 multiply_reduce_fusion
  1.9 1.1 slice_bitcast_fusion.3
  3.0 1.0 slice_reduce_fusion.1
  4.6 0.6 fusion.48
  5.2 0.6 fusion.47
  5.9 3.1 %collective-permute-start = (f32[4,16,16,128]{3,2,1,0:T(8,128)S(1)}, f32[4,16,16,128]{3,2,1,0:T(8,128)S(1)}, u32[]{:S(2)}, u32[]{:S(2)}) collective-permute-start(f32[4,16,16,128]{3,2,1,0:T(8,128)S(1)} %get-tuple-element.26), channel_id=1, source_target_pairs={{0,1},{1,2},{2,3},{3,4},{4,5},{5,6},{6,7},{7,8},{8,9},{9,10},{10,1... | collective-permute-start | bytes 1572872 | tf_op jit(solution)/shard_map/ppermute | solution.py:22
  9.1 2.2 %collective-permute-start.1 = (f32[4,16,16,128]{3,2,1,0:T(8,128)S(1)}, f32[4,16,16,128]{3,2,1,0:T(8,128)S(1)}, u32[]{:S(2)}, u32[]{:S(2)}) collective-permute-start(f32[4,16,16,128]{3,2,1,0:T(8,128)S(1)} %get-tuple-element.27), channel_id=1, source_target_pairs={{1,0},{2,1},{3,2},{4,3},{5,4},{6,5},{7,6},{8,7},{9,8},{10,9},{11,1... | collective-permute-start | bytes 1572872 | tf_op jit(solution)/shard_map/ppermute | solution.py:24
  11.2 9.4 %collective-permute-done = f32[4,16,16,128]{3,2,1,0:T(8,128)S(1)} collective-permute-done((f32[4,16,16,128]{3,2,1,0:T(8,128)S(1)}, f32[4,16,16,128]{3,2,1,0:T(8,128)S(1)}, u32[]{:S(2)}, u32[]{:S(2)}) %collective-permute-start) | collective-permute-done | bytes 524320 | tf_op jit(solution)/shard_map/ppermute | solution.py:22
  20.6 5.0 %collective-permute-done.1 = f32[4,16,16,128]{3,2,1,0:T(8,128)S(1)} collective-permute-done((f32[4,16,16,128]{3,2,1,0:T(8,128)S(1)}, f32[4,16,16,128]{3,2,1,0:T(8,128)S(1)}, u32[]{:S(2)}, u32[]{:S(2)}) %collective-permute-start.1) | collective-permute-done | bytes 524320 | tf_op jit(solution)/shard_map/ppermute | solution.py:24
  25.6 0.7 convolution_bitcast_fusion.6
  26.3 0.7 convolution_bitcast_fusion.4
  27.0 0.7 convolution_bitcast_fusion.5
  27.8 1.3 pad_maximum_fusion.3
  29.1 6.4 %collective-permute-start.2 = (f32[6,16,32,128]{3,2,1,0:T(8,128)}, f32[6,16,32,128]{3,2,1,0:T(8,128)}, u32[]{:S(2)}, u32[]{:S(2)}) collective-permute-start(f32[6,16,32,128]{3,2,1,0:T(8,128)} %pad_maximum_fusion.3), channel_id=1, source_target_pairs={{0,16},{16,32},{32,48},{48,64},{64,80},{80,96},{96,112},{112,128},... | collective-permute-start | bytes 4718600 | tf_op jit(solution)/shard_map/ppermute | solution.py:22
  35.6 1.9 %collective-permute-start.3 = (f32[6,16,32,128]{3,2,1,0:T(8,128)}, f32[6,16,32,128]{3,2,1,0:T(8,128)}, u32[]{:S(2)}, u32[]{:S(2)}) collective-permute-start(f32[6,16,32,128]{3,2,1,0:T(8,128)} %pad_maximum_fusion.3), channel_id=1, source_target_pairs={{16,0},{32,16},{48,32},{64,48},{80,64},{96,80},{112,96},{128,112},... | collective-permute-start | bytes 4718600 | tf_op jit(solution)/shard_map/ppermute | solution.py:24
  38.6 14.6 %collective-permute-done.2 = f32[6,16,32,128]{3,2,1,0:T(8,128)} collective-permute-done((f32[6,16,32,128]{3,2,1,0:T(8,128)}, f32[6,16,32,128]{3,2,1,0:T(8,128)}, u32[]{:S(2)}, u32[]{:S(2)}) %collective-permute-start.2) | collective-permute-done | bytes 1572896 | tf_op jit(solution)/shard_map/ppermute | solution.py:22
  53.2 5.6 %collective-permute-done.3 = f32[6,16,32,128]{3,2,1,0:T(8,128)} collective-permute-done((f32[6,16,32,128]{3,2,1,0:T(8,128)}, f32[6,16,32,128]{3,2,1,0:T(8,128)}, u32[]{:S(2)}, u32[]{:S(2)}) %collective-permute-start.3) | collective-permute-done | bytes 1572896 | tf_op jit(solution)/shard_map/ppermute | solution.py:24
  58.8 2.7 %pad_maximum_fusion = f32[6,48,32,128]{3,2,1,0:T(8,128)S(1)} fusion(f32[6,16,32,128]{3,2,1,0:T(8,128)} %collective-permute-done.3, f32[2,16,32,128]{3,2,1,0:T(8,128)} %copy-done.3, f32[2,16,32,128]{3,2,1,0:T(8,128)} %copy-done.4, f32[2,16,32,128]{3,2,1,0:T(8,128)} %copy-done.2, f32[6,16,32,128]{3,2,1,0:T(8,128)} %collective-permute-done.2), kind=kLoop, calls=%fused_computation | loop fusion | flops 4718592 | bytes 9437184 | tf_op jit(solution)/shard_map/concatenate | solution.py:20
  61.5 1.0 fusion.194
  62.5 1.8 %fusion.8 = f32[2,16,32,128]{3,1,2,0:T(8,128)S(1)} fusion(f32[2,48,32,128]{3,2,1,0:T(8,128)S(1)} %get-tuple-element.15, f32[]{:T(128)S(6)} %sqrt.20), kind=kOutput, calls=%fused_computation.22 | convolution fusion | flops 75505920 | bytes 2097156 | tf_op jit(solution)/shard_map/ck,fkyz->fcyz/dot_general | solution.py:53
  64.4 1.8 %fusion.11 = f32[2,16,32,128]{3,1,2,0:T(8,128)S(1)} fusion(f32[2,48,32,128]{3,2,1,0:T(8,128)S(1)} %get-tuple-element.14, f32[]{:T(128)S(6)} %sqrt.19), kind=kOutput, calls=%fused_computation.23 | convolution fusion | flops 75504384 | bytes 2097156 | tf_op jit(solution)/shard_map/ck,fkyz->fcyz/dot_general | solution.py:53
  66.4 1.9 %collective-permute-start.4 = (f32[8,1,32,128]{3,1,2,0:T(1,128)S(1)}, f32[8,1,32,128]{3,1,2,0:T(1,128)S(1)}, u32[]{:S(2)}, u32[]{:S(2)}) collective-permute-start(f32[8,1,32,128]{3,1,2,0:T(1,128)S(1)} %get-tuple-element.21), channel_id=1, source_target_pairs={{16,0},{32,16},{48,32},{64,48},{80,64},{96,80},{112,96},{128,112},... | collective-permute-start | bytes 393224 | tf_op jit(solution)/shard_map/ppermute | solution.py:24
  68.3 5.0 %collective-permute-start.5 = (f32[8,1,32,128]{3,1,2,0:T(1,128)S(1)}, f32[8,1,32,128]{3,1,2,0:T(1,128)S(1)}, u32[]{:S(2)}, u32[]{:S(2)}) collective-permute-start(f32[8,1,32,128]{3,1,2,0:T(1,128)S(1)} %get-tuple-element.20), channel_id=1, source_target_pairs={{0,16},{16,32},{32,48},{48,64},{64,80},{80,96},{96,112},{112,128},... | collective-permute-start | bytes 393224 | tf_op jit(solution)/shard_map/ppermute | solution.py:22
  73.4 1.8 %fusion.14 = f32[2,16,32,128]{3,1,2,0:T(8,128)S(1)} fusion(f32[2,48,32,128]{3,2,1,0:T(8,128)S(1)} %get-tuple-element.13, f32[]{:T(128)S(6)} %sqrt.19), kind=kOutput, calls=%fused_computation.24 | convolution fusion | flops 75504384 | bytes 2097156 | tf_op jit(solution)/shard_map/ck,fkyz->fcyz/dot_general | solution.py:53
  75.4 0.9 subtract_multiply_fusion.2
  76.3 1.5 %convolution_bitcast_fusion = f32[2,48,32,128]{3,1,2,0:T(8,128)S(1)} fusion(f32[2,16,32,128]{3,1,2,0:T(8,128)S(1)} %get-tuple-element.9, f32[2,16,32,127]{3,1,2,0:T(8,128)S(1)} %bitcast.85, f32[]{:T(128)S(6)} %sqrt.19), kind=kOutput, calls=%fused_computation.16 | convolution fusion | flops 75766528 | bytes 2617348 | tf_op jit(solution)/shard_map/ck,fkyz->fcyz/dot_general | solution.py:53
  77.8 1.9 %collective-permute-start.6 = (f32[8,18,1,128]{3,1,2,0:T(8,128)S(1)}, f32[8,18,1,128]{3,1,2,0:T(8,128)S(1)}, u32[]{:S(2)}, u32[]{:S(2)}) collective-permute-start(f32[8,18,1,128]{3,1,2,0:T(8,128)S(1)} %get-tuple-element.16), channel_id=1, source_target_pairs={{1,0},{2,1},{3,2},{4,3},{5,4},{6,5},{7,6},{8,7},{9,8},{10,9},{11,1... | collective-permute-start | bytes 221192 | tf_op jit(solution)/shard_map/ppermute | solution.py:24
  79.8 5.5 %collective-permute-start.7 = (f32[8,18,1,128]{3,1,2,0:T(8,128)S(1)}, f32[8,18,1,128]{3,1,2,0:T(8,128)S(1)}, u32[]{:S(2)}, u32[]{:S(2)}) collective-permute-start(f32[8,18,1,128]{3,1,2,0:T(8,128)S(1)} %get-tuple-element.17), channel_id=1, source_target_pairs={{0,1},{1,2},{2,3},{3,4},{4,5},{5,6},{6,7},{7,8},{8,9},{9,10},{10,1... | collective-permute-start | bytes 221192 | tf_op jit(solution)/shard_map/ppermute | solution.py:22
  85.2 2.3 %subtract_multiply_fusion = f32[2,17,32,128]{3,1,2,0:T(8,128)S(1)} fusion(f32[2,16,32,128]{3,1,2,0:T(8,128)S(1)} %fusion.11, f32[2,16,32,128]{3,1,2,0:T(8,128)S(1)} %fusion.8, f32[2,16,32,128]{3,1,2,0:T(8,128)S(1)} %copy.11, f32[2,16,32,128]{3,1,2,0:T(8,128)S(1)} %copy.6, f32[8,1,32,128]{3,1,2,0:T(1,128)S(1)} %collective-permute-done.5, ...), kind=kLoop, calls=%fused_computation.46 | loop fusion | flops 5431296 | bytes 2916369 | tf_op jit(solution)/shard_map/mul | solution.py:72
  87.6 1.4 convolution_bitcast_fusion.2
  89.0 1.4 subtract_multiply_fusion.1
  90.5 1.4 convolution_bitcast_fusion.1
  92.7 3.5 %collective-permute-start.8 = (f32[6,16,32,128]{3,1,2,0:T(8,128)S(1)}, f32[6,16,32,128]{3,1,2,0:T(8,128)S(1)}, u32[]{:S(2)}, u32[]{:S(2)}) collective-permute-start(f32[6,16,32,128]{3,1,2,0:T(8,128)S(1)} %get-tuple-element.11), channel_id=1, source_target_pairs={{0,16},{16,32},{32,48},{48,64},{64,80},{80,96},{96,112},{112,128},... | collective-permute-start | bytes 4718600 | tf_op jit(solution)/shard_map/ppermute | solution.py:22
  96.2 2.1 %collective-permute-start.9 = (f32[6,16,32,128]{3,1,2,0:T(8,128)S(1)}, f32[6,16,32,128]{3,1,2,0:T(8,128)S(1)}, u32[]{:S(2)}, u32[]{:S(2)}) collective-permute-start(f32[6,16,32,128]{3,1,2,0:T(8,128)S(1)} %get-tuple-element.12), channel_id=1, source_target_pairs={{16,0},{32,16},{48,32},{64,48},{80,64},{96,80},{112,96},{128,112},... | collective-permute-start | bytes 4718600 | tf_op jit(solution)/shard_map/ppermute | solution.py:24
  98.9 14.5 %collective-permute-done.8 = f32[6,16,32,128]{3,1,2,0:T(8,128)S(1)} collective-permute-done((f32[6,16,32,128]{3,1,2,0:T(8,128)S(1)}, f32[6,16,32,128]{3,1,2,0:T(8,128)S(1)}, u32[]{:S(2)}, u32[]{:S(2)}) %collective-permute-start.8) | collective-permute-done | bytes 1572896 | tf_op jit(solution)/shard_map/ppermute | solution.py:22
  113.5 5.6 %collective-permute-done.9 = f32[6,16,32,128]{3,1,2,0:T(8,128)S(1)} collective-permute-done((f32[6,16,32,128]{3,1,2,0:T(8,128)S(1)}, f32[6,16,32,128]{3,1,2,0:T(8,128)S(1)}, u32[]{:S(2)}, u32[]{:S(2)}) %collective-permute-start.9) | collective-permute-done | bytes 1572896 | tf_op jit(solution)/shard_map/ppermute | solution.py:24
  119.6 1.1 fusion.41
  120.7 1.1 convolution_bitcast_fusion.3
  121.8 1.1 fusion.7
  123.0 4.5 %collective-permute-start.10 = (f32[4,16,16,128]{3,2,1,0:T(8,128)S(1)}, f32[4,16,16,128]{3,2,1,0:T(8,128)S(1)}, u32[]{:S(2)}, u32[]{:S(2)}) collective-permute-start(f32[4,16,16,128]{3,2,1,0:T(8,128)S(1)} %get-tuple-element.18), channel_id=1, source_target_pairs={{0,1},{1,2},{2,3},{3,4},{4,5},{5,6},{6,7},{7,8},{8,9},{9,10},{10,1... | collective-permute-start | bytes 1572872 | tf_op jit(solution)/shard_map/ppermute | solution.py:22
  127.6 1.9 %collective-permute-start.11 = (f32[4,16,16,128]{3,2,1,0:T(8,128)S(1)}, f32[4,16,16,128]{3,2,1,0:T(8,128)S(1)}, u32[]{:S(2)}, u32[]{:S(2)}) collective-permute-start(f32[4,16,16,128]{3,2,1,0:T(8,128)S(1)} %get-tuple-element.19), channel_id=1, source_target_pairs={{1,0},{2,1},{3,2},{4,3},{5,4},{6,5},{7,6},{8,7},{9,8},{10,9},{11,1... | collective-permute-start | bytes 1572872 | tf_op jit(solution)/shard_map/ppermute | solution.py:24
  130.2 5.0 %collective-permute-done.10 = f32[4,16,16,128]{3,2,1,0:T(8,128)S(1)} collective-permute-done((f32[4,16,16,128]{3,2,1,0:T(8,128)S(1)}, f32[4,16,16,128]{3,2,1,0:T(8,128)S(1)}, u32[]{:S(2)}, u32[]{:S(2)}) %collective-permute-start.10) | collective-permute-done | bytes 524320 | tf_op jit(solution)/shard_map/ppermute | solution.py:22
  135.2 6.0 %collective-permute-done.11 = f32[4,16,16,128]{3,2,1,0:T(8,128)S(1)} collective-permute-done((f32[4,16,16,128]{3,2,1,0:T(8,128)S(1)}, f32[4,16,16,128]{3,2,1,0:T(8,128)S(1)}, u32[]{:S(2)}, u32[]{:S(2)}) %collective-permute-start.11) | collective-permute-done | bytes 524320 | tf_op jit(solution)/shard_map/ppermute | solution.py:24
  141.2 0.6 fusion.60
  141.8 0.6 convolution_add_fusion.1
  142.7 1.0 fusion.37
  143.7 1.0 copy.20
  (43 shorter events, 4.6 us)
Async XLA Ops:
  5.9 14.7 %collective-permute-start = (f32[4,16,16,128]{3,2,1,0:T(8,128)S(1)}, f32[4,16,16,128]{3,2,1,0:T(8,128)S(1)}, u32[]{:S(2)}, u32[]{:S(2)}) collective-permute-start(f32[4,16,16,128]{3,2,1,0:T(8,128)S(1)} %get-tuple-element.26), channel_id=1, source_target_pairs={{0,1},{1,2},{2,3},{3,4},{4,5},{5,6},{6,7},{7,8},{8,9},{9,10},{10,1... | collective-permute-start | bytes 1572872 | tf_op jit(solution)/shard_map/ppermute | solution.py:22
  9.1 16.5 %collective-permute-start.1 = (f32[4,16,16,128]{3,2,1,0:T(8,128)S(1)}, f32[4,16,16,128]{3,2,1,0:T(8,128)S(1)}, u32[]{:S(2)}, u32[]{:S(2)}) collective-permute-start(f32[4,16,16,128]{3,2,1,0:T(8,128)S(1)} %get-tuple-element.27), channel_id=1, source_target_pairs={{1,0},{2,1},{3,2},{4,3},{5,4},{6,5},{7,6},{8,7},{9,8},{10,9},{11,1... | collective-permute-start | bytes 1572872 | tf_op jit(solution)/shard_map/ppermute | solution.py:24
  26.3 1.5 %copy-start.2 = (f32[2,16,32,128]{3,2,1,0:T(8,128)}, f32[2,16,32,128]{3,2,1,0:T(8,128)S(1)}, u32[]{:S(2)}) copy-start(f32[2,16,32,128]{3,2,1,0:T(8,128)S(1)} %convolution_bitcast_fusion.6) | copy-start | bytes 1572868
  27.0 2.1 %copy-start.3 = (f32[2,16,32,128]{3,2,1,0:T(8,128)}, f32[2,16,32,128]{3,2,1,0:T(8,128)S(1)}, u32[]{:S(2)}) copy-start(f32[2,16,32,128]{3,2,1,0:T(8,128)S(1)} %convolution_bitcast_fusion.4) | copy-start | bytes 1572868
  27.7 1.4 copy-start.4
  27.8 9.7 %copy-start.1 = (f32[2,16,32,128]{3,2,1,0:T(8,128)S(1)}, f32[2,16,32,128]{3,2,1,0:T(8,128)}, u32[]{:S(2)}) copy-start(f32[2,16,32,128]{3,2,1,0:T(8,128)} %param.3) | copy-start | bytes 1572868
  27.8 10.0 %copy-start = (f32[2,16,32,128]{3,2,1,0:T(8,128)S(1)}, f32[2,16,32,128]{3,2,1,0:T(8,128)}, u32[]{:S(2)}) copy-start(f32[2,16,32,128]{3,2,1,0:T(8,128)} %param.4) | copy-start | bytes 1572868
  29.1 24.1 %collective-permute-start.2 = (f32[6,16,32,128]{3,2,1,0:T(8,128)}, f32[6,16,32,128]{3,2,1,0:T(8,128)}, u32[]{:S(2)}, u32[]{:S(2)}) collective-permute-start(f32[6,16,32,128]{3,2,1,0:T(8,128)} %pad_maximum_fusion.3), channel_id=1, source_target_pairs={{0,16},{16,32},{32,48},{48,64},{64,80},{80,96},{96,112},{112,128},... | collective-permute-start | bytes 4718600 | tf_op jit(solution)/shard_map/ppermute | solution.py:22
  35.6 23.3 %collective-permute-start.3 = (f32[6,16,32,128]{3,2,1,0:T(8,128)}, f32[6,16,32,128]{3,2,1,0:T(8,128)}, u32[]{:S(2)}, u32[]{:S(2)}) collective-permute-start(f32[6,16,32,128]{3,2,1,0:T(8,128)} %pad_maximum_fusion.3), channel_id=1, source_target_pairs={{16,0},{32,16},{48,32},{64,48},{80,64},{96,80},{112,96},{128,112},... | collective-permute-start | bytes 4718600 | tf_op jit(solution)/shard_map/ppermute | solution.py:24
  66.4 11.4 %collective-permute-start.4 = (f32[8,1,32,128]{3,1,2,0:T(1,128)S(1)}, f32[8,1,32,128]{3,1,2,0:T(1,128)S(1)}, u32[]{:S(2)}, u32[]{:S(2)}) collective-permute-start(f32[8,1,32,128]{3,1,2,0:T(1,128)S(1)} %get-tuple-element.21), channel_id=1, source_target_pairs={{16,0},{32,16},{48,32},{64,48},{80,64},{96,80},{112,96},{128,112},... | collective-permute-start | bytes 393224 | tf_op jit(solution)/shard_map/ppermute | solution.py:24
  68.3 9.4 %collective-permute-start.5 = (f32[8,1,32,128]{3,1,2,0:T(1,128)S(1)}, f32[8,1,32,128]{3,1,2,0:T(1,128)S(1)}, u32[]{:S(2)}, u32[]{:S(2)}) collective-permute-start(f32[8,1,32,128]{3,1,2,0:T(1,128)S(1)} %get-tuple-element.20), channel_id=1, source_target_pairs={{0,16},{16,32},{32,48},{48,64},{64,80},{80,96},{96,112},{112,128},... | collective-permute-start | bytes 393224 | tf_op jit(solution)/shard_map/ppermute | solution.py:22
  77.8 11.2 %collective-permute-start.6 = (f32[8,18,1,128]{3,1,2,0:T(8,128)S(1)}, f32[8,18,1,128]{3,1,2,0:T(8,128)S(1)}, u32[]{:S(2)}, u32[]{:S(2)}) collective-permute-start(f32[8,18,1,128]{3,1,2,0:T(8,128)S(1)} %get-tuple-element.16), channel_id=1, source_target_pairs={{1,0},{2,1},{3,2},{4,3},{5,4},{6,5},{7,6},{8,7},{9,8},{10,9},{11,1... | collective-permute-start | bytes 221192 | tf_op jit(solution)/shard_map/ppermute | solution.py:24
  79.8 9.3 %collective-permute-start.7 = (f32[8,18,1,128]{3,1,2,0:T(8,128)S(1)}, f32[8,18,1,128]{3,1,2,0:T(8,128)S(1)}, u32[]{:S(2)}, u32[]{:S(2)}) collective-permute-start(f32[8,18,1,128]{3,1,2,0:T(8,128)S(1)} %get-tuple-element.17), channel_id=1, source_target_pairs={{0,1},{1,2},{2,3},{3,4},{4,5},{5,6},{6,7},{7,8},{8,9},{9,10},{10,1... | collective-permute-start | bytes 221192 | tf_op jit(solution)/shard_map/ppermute | solution.py:22
  92.5 5.8 %copy-start.5 = (f32[2,2]{1,0:T(2,128)S(1)}, f32[2,2]{1,0:T(2,128)}, u32[]{:S(2)}) copy-start(f32[2,2]{1,0:T(2,128)} %param.5) | copy-start | bytes 52
  92.7 20.8 %collective-permute-start.8 = (f32[6,16,32,128]{3,1,2,0:T(8,128)S(1)}, f32[6,16,32,128]{3,1,2,0:T(8,128)S(1)}, u32[]{:S(2)}, u32[]{:S(2)}) collective-permute-start(f32[6,16,32,128]{3,1,2,0:T(8,128)S(1)} %get-tuple-element.11), channel_id=1, source_target_pairs={{0,16},{16,32},{32,48},{48,64},{64,80},{80,96},{96,112},{112,128},... | collective-permute-start | bytes 4718600 | tf_op jit(solution)/shard_map/ppermute | solution.py:22
  96.2 22.9 %collective-permute-start.9 = (f32[6,16,32,128]{3,1,2,0:T(8,128)S(1)}, f32[6,16,32,128]{3,1,2,0:T(8,128)S(1)}, u32[]{:S(2)}, u32[]{:S(2)}) collective-permute-start(f32[6,16,32,128]{3,1,2,0:T(8,128)S(1)} %get-tuple-element.12), channel_id=1, source_target_pairs={{16,0},{32,16},{48,32},{64,48},{80,64},{96,80},{112,96},{128,112},... | collective-permute-start | bytes 4718600 | tf_op jit(solution)/shard_map/ppermute | solution.py:24
  123.0 12.2 %collective-permute-start.10 = (f32[4,16,16,128]{3,2,1,0:T(8,128)S(1)}, f32[4,16,16,128]{3,2,1,0:T(8,128)S(1)}, u32[]{:S(2)}, u32[]{:S(2)}) collective-permute-start(f32[4,16,16,128]{3,2,1,0:T(8,128)S(1)} %get-tuple-element.18), channel_id=1, source_target_pairs={{0,1},{1,2},{2,3},{3,4},{4,5},{5,6},{6,7},{7,8},{8,9},{9,10},{10,1... | collective-permute-start | bytes 1572872 | tf_op jit(solution)/shard_map/ppermute | solution.py:22
  127.6 13.6 %collective-permute-start.11 = (f32[4,16,16,128]{3,2,1,0:T(8,128)S(1)}, f32[4,16,16,128]{3,2,1,0:T(8,128)S(1)}, u32[]{:S(2)}, u32[]{:S(2)}) collective-permute-start(f32[4,16,16,128]{3,2,1,0:T(8,128)S(1)} %get-tuple-element.19), channel_id=1, source_target_pairs={{1,0},{2,1},{3,2},{4,3},{5,4},{6,5},{7,6},{8,7},{9,8},{10,9},{11,1... | collective-permute-start | bytes 1572872 | tf_op jit(solution)/shard_map/ppermute | solution.py:24
where the time goes:
time: 145 us
  waiting for transfers between devices  65.7 us (45%)
  starting transfers between devices  40 us (28%)
  matrix products  17.6 us (12%)
  other arithmetic  13.6 us (9%)
  local copies, waits for them, and re-layouts  5.91 us (4%)
  between operations  1.86 us (1%)
    ppermute x6, waiting for transfers between devices, padded(): lax.ppermute(tail, axis, [(i, (i + 1) % count) for i in range(ends)])  43.6 us
    ppermute x6, starting transfers between devices, padded(): lax.ppermute(tail, axis, [(i, (i + 1) % count) for i in range(ends)])  28 us
    ppermute x6, waiting for transfers between devices, padded(): lax.ppermute(head, axis, [((i + 1) % count, i) for i in range(ends)])  22.1 us
    ppermute x6, starting transfers between devices, padded(): lax.ppermute(head, axis, [((i + 1) % count, i) for i in range(ends)])  12 us
    dot_general x6, matrix products, along_x(): return jnp.einsum('ck,fkyz->fcyz', matrix, values, precision=highest)  9.78 us
    dot_general x6, matrix products, along_y(): return jnp.einsum('ck,fxkz->fxcz', matrix, values, precision=highest)  5.38 us
    mul x3, other arithmetic, face_terms(): flux_bar * (0.5 * (lower_density + upper_density) - 0.5 * face_velocity /...  4.63 us
  transfers between devices with their start and end apart: 12, of which 8 were waited for; matrix products, arithmetic and copies ran while one was open for 7% of the time, Pallas kernels for 0%

commit v1 on v0

v1 whole, which is shorter than its diff:
```python
import jax
import jax.numpy as jnp
import numpy as np
from jax import lax
from jax.experimental import pallas as pl
from jax.experimental.pallas import tpu as pltpu
from jax.sharding import PartitionSpec as P


R = 16
W = R + 1
NX = 16
NY = 32
NZ = 128
f32 = jnp.float32
bf16 = jnp.bfloat16

SMOOTH2 = 0.01
STEP = 0.5

offs = np.arange(-R, R + 1).astype(np.float64)
even_norm = np.sqrt(np.sum((W - np.abs(offs)) ** 2))
odd_norm = np.sqrt(np.sum((offs * (W - np.abs(offs))) ** 2))
SCALE = float(1.0 / (even_norm * even_norm * odd_norm))


def even(d):
    return np.where(np.abs(d) <= R, W - np.abs(d), 0).astype(np.float32)


def odd(d):
    return np.where(np.abs(d) <= R, d * (W - np.abs(d)), 0).astype(np.float32)


def y_matrix():
    lines = np.full(80, 10**6)
    lines[0:64] = np.arange(-16, 48)
    lines[64] = -17
    lines[65] = 48
    m = np.zeros((80, 80), np.float32)
    for c in range(NY):
        m[c] = even(lines - c)
    for j in range(NY + 1):
        m[NY + j] = odd(lines - (j - 1)) + odd(lines - j)
    return np.concatenate([m, m], 1)


def y_transposed():
    k = np.arange(-16, 48)[:, None]
    c = np.arange(NY)[None, :]
    m = np.concatenate([even(k - c), odd(k - c)], 1)
    return np.concatenate([m, m], 1)


def z_matrices():
    k = np.arange(NZ)[:, None]
    j = np.arange(NZ)[None, :]
    ze = even(k - j)
    zo = odd(k - j) + odd(k - j - 1)
    zo[:, NZ - 1] = 0
    return [np.concatenate([m, m], 0) for m in (ze, zo, zo.T)]


def split(x):
    hi = x.astype(bf16)
    lo = (x - hi.astype(f32)).astype(bf16)
    return hi, lo


def dot(a, b):
    return jnp.dot(a, b, preferred_element_type=f32)


def dot_rows(x, m):
    hi, lo = split(x)
    return dot(jnp.concatenate([hi, lo], 1), m)


YROWS = 576
CROWS = 544 * 2 + 64


def scalars_kernel(info, adh, info_out, adh_out):
    for i in range(5):
        info_out[i] = info[i]
    for i in range(2):
        for j in range(2):
            adh_out[i, j] = adh[i, j]


def pack_kernel(d, c, up, dn):
    for n in range(32):
        up[n * 16 : n * 16 + 16, :] = d[n * 32 + 16 : n * 32 + 32, :]
        dn[n * 16 : n * 16 + 16, :] = d[n * 32 : n * 32 + 16, :]
    up[512:544, :] = d[pl.ds(15, 32, stride=32), :]
    dn[512:544, :] = d[pl.ds(16, 32, stride=32), :]
    up[544:576, :] = c[pl.ds(31, 32, stride=32), :]
    dn[544:576, :] = c[pl.ds(0, 32, stride=32), :]


def corner_kernel(info, d, c, yl, yr, ma, mb, e0, e15):
    edge = info[0]
    for ref in (ma, mb):
        ref[0:544, :] = yl[0:544, :]
        ref[544:1088, :] = yr[0:544, :]
    for p in range(2):
        near = pl.multiple_of(p * 512 + (1 - edge) * 480, 32)
        far = pl.multiple_of(p * 512 + edge * 480, 32)
        r = 1088 + p * 32
        ma[r : r + 32, :] = c[pl.ds(near, 32), :]
        mb[r : r + 32, :] = c[pl.ds(far, 32), :]
        for ref, x in ((e0, 0), (e15, NX - 1)):
            n = p * 16 + x
            ref[p * 64 : p * 64 + 16, :] = yl[n * 16 : n * 16 + 16, :]
            ref[p * 64 + 16 : p * 64 + 48, :] = d[n * 32 : n * 32 + 32, :]
            ref[p * 64 + 48 : p * 64 + 64, :] = yr[n * 16 : n * 16 + 16, :]


def face(f, dl, du, cl, cu, valid):
    g = f * f + SMOOTH2
    r = lax.rsqrt(g)
    mag = g * r
    fb = (0.5 * STEP) * (cu - cl)
    if valid is not None:
        fb = jnp.where(valid, fb, 0.0)
    lower = fb * (f + mag)
    upper = fb * (f - mag)
    vb = fb * ((dl + du) - (f * r) * (du - dl))
    return lower, upper, vb


def main_kernel(
    info, adh, d, c, yl, yr, ba, bb, ka, kb, r2l, r2r, my, ze, zo, zot, myt,
    base, own, low, high, ga, gb, ha, hb,
    se, so, s1, s2, xo, xe, xy, dy, cy, tly, vby, wx, wy, wz, edges, ext, gm, hm,
):
    odd_core = info[0]
    left, right = info[1], info[2]
    below, above = info[3], info[4]

    a00, a01, a10, a11 = adh[0, 0], adh[0, 1], adh[1, 0], adh[1, 1]
    mat = my[...]

    def y_filter(parts):
        both = jnp.concatenate(
            [a00 * parts[0] + a01 * parts[1], a10 * parts[0] + a11 * parts[1]], 1
        )
        hi, lo = split(both)
        return dot(mat, jnp.concatenate([hi, lo], 0))

    ext[...] = jnp.zeros((1536, 128), f32)
    blocks = (
        (d, yl, 0, yr, 0, 16),
        (ba, ka, 0, ka, 544, 32 - 32 * odd_core),
        (bb, kb, 0, kb, 544, 32 * odd_core),
    )
    for i, (blk, kl, ol, kr, oh, first) in enumerate(blocks):
        ext[pl.ds(i * 512, 32, stride=16), :] = kl[ol + 512 : ol + 544, :]
        ext[pl.ds(i * 512 + 1, 32, stride=16), :] = kr[oh + 512 : oh + 544, :]
        for x in range(NX):
            parts = []
            for p in range(2):
                n = p * 16 + x
                r = i * 512 + n * 16
                parts.append(
                    jnp.concatenate(
                        [
                            kl[ol + n * 16 : ol + n * 16 + 16, :],
                            blk[n * 32 : n * 32 + 32, :],
                            kr[oh + n * 16 : oh + n * 16 + 16, :],
                            ext[r : r + 16, :],
                        ],
                        0,
                    )
                )
            out = y_filter(parts)
            for p in range(2):
                z = slice(p * 128, p * 128 + 128)
                re = (first + 1 + x) * 64 + p * 32
                ro = (first + x) * 80 + p * 40
                if i:
                    re, ro = pl.multiple_of(re, 32), pl.multiple_of(ro, 8)
                se[pl.ds(re, 32), :] = out[0:32, z]
                so[pl.ds(ro, 40), :] = out[32:72, z]
    for ref, q in ((r2l, 0), (r2r, 49)):
        zero16 = jnp.zeros((16, 128), f32)
        parts = [jnp.concatenate([ref[p * 64 : p * 64 + 64, :], zero16], 0) for p in range(2)]
        out = y_filter(parts)
        for p in range(2):
            se[q * 64 + p * 32 : q * 64 + p * 32 + 32, :] = out[0:32, p * 128 : p * 128 + 128]
    for ref, kref, side in ((ba, ka, 1 - odd_core), (bb, kb, odd_core)):
        q = pl.multiple_of(side * 128, 128)
        for p in range(2):
            src = pl.multiple_of(p * 512 + (1 - side) * 480, 32)
            edges[pl.ds(q + p * 32, 32), :] = ref[pl.ds(src, 32), :]
        edges[pl.ds(q + 64, 64), :] = kref[1088:1152, :]

    def pe(plane):
        q = (plane + 17) * 64
        return se[q : q + 64, :]

    def po(plane):
        q = (plane + 16) * 80
        return so[q : q + 80, :]

    b = pe(-17)
    for k in range(-16, 0):
        b = b + pe(k)
    t = None
    for j in range(1, 9):
        term = float(j) * (pe(-9 + j) - pe(-9 - j))
        t = term if t is None else t + term
    s2[0:64, :] = t
    for m in range(-9, 24):
        new, old = pe(m + 9), pe(m - 8)
        t = t + (8.0 * (new + old) + (old - b))
        s2[(m + 10) * 64 : (m + 11) * 64, :] = t
        if m < 23:
            b = b + (new - old)
            s1[(m + 9) * 64 : (m + 10) * 64, :] = b
    e = s1[0:64, :]
    for m in range(1, 17):
        e = e + s1[m * 64 : m * 64 + 64, :]
    xe[0:64, :] = e
    for k in range(15):
        e = e + (s1[(k + 17) * 64 : (k + 18) * 64, :] - s1[k * 64 : k * 64 + 64, :])
        xe[(k + 1) * 64 : (k + 2) * 64, :] = e
    o = s2[0:64, :]
    for m in range(1, 17):
        o = o + s2[m * 64 : m * 64 + 64, :]
    for j in range(17):
        nxt = o + (s2[(j + 17) * 64 : (j + 18) * 64, :] - s2[j * 64 : j * 64 + 64, :])
        xo[j * 64 : j * 64 + 64, :] = o + nxt
        o = nxt
    b = po(-16)
    for k in range(-15, 1):
        b = b + po(k)
    s1[0:80, :] = b
    for m in range(-8, 23):
        b = b + (po(m + 9) - po(m - 8))
        s1[(m + 9) * 80 : (m + 10) * 80, :] = b
    e = s1[0:80, :]
    for m in range(1, 17):
        e = e + s1[m * 80 : m * 80 + 80, :]
    xy[0:80, :] = e
    for k in range(15):
        e = e + (s1[(k + 17) * 80 : (k + 18) * 80, :] - s1[k * 80 : k * 80 + 80, :])
        xy[(k + 1) * 80 : (k + 2) * 80, :] = e

    mze, mzo, mzot = ze[...], zo[...], zot[...]
    for r in range(0, 1088, 64):
        xo[r : r + 64, :] = dot_rows(xo[r : r + 64, :], mze)
    for r in range(0, 1280, 80):
        xy[r : r + 80, :] = dot_rows(xy[r : r + 80, :], mze)
    for r in range(0, 1024, 64):
        xe[r : r + 64, :] = dot_rows(xe[r : r + 64, :], mzo)

    for p in range(2):
        prev_upper = prev_vb = None
        for j in range(17):
            f = SCALE * xo[j * 64 + p * 32 : j * 64 + p * 32 + 32, :]
            lo = p * 512 + (j - 1) * 32
            hi = p * 512 + j * 32
            dl = edges[p * 32 : p * 32 + 32, :] if j == 0 else d[lo : lo + 32, :]
            cl = edges[64 + p * 32 : 96 + p * 32, :] if j == 0 else c[lo : lo + 32, :]
            du = edges[128 + p * 32 : 160 + p * 32, :] if j == 16 else d[hi : hi + 32, :]
            cu = edges[192 + p * 32 : 224 + p * 32, :] if j == 16 else c[hi : hi + 32, :]
            valid = {0: left, 16: right}.get(j)
            lower, upper, vb = face(f, dl, du, cl, cu, None if valid is None else valid == 1)
            if j:
                base[lo : lo + 32, :] = cl + (lower + prev_upper)
                r = (j - 1) * 64 + p * 32
                wx[r : r + 32, :] = vb + prev_vb
            prev_upper, prev_vb = upper, vb

    for p in range(2):
        q = p * 16
        dy[pl.ds(p * 48 + 7, 16, stride=96), :] = yl[pl.ds(p * 256 + 15, 16, stride=16), :]
        dy[pl.ds(p * 48 + 40, 16, stride=96), :] = yr[pl.ds(p * 256, 16, stride=16), :]
        cy[pl.ds(p * 48 + 7, 16, stride=96), :] = yl[544 + q : 560 + q, :]
        cy[pl.ds(p * 48 + 40, 16, stride=96), :] = yr[544 + q : 560 + q, :]
        for x in range(NX):
            s = p * 512 + x * 32
            t = (x * 2 + p) * 48 + 8
            dy[t : t + 32, :] = d[s : s + 32, :]
            cy[t : t + 32, :] = c[s : s + 32, :]
    row = lax.broadcasted_iota(jnp.int32, (40, 128), 0)
    valid_y = ((row > 0) | (below == 1)) & ((row < 32) | (above == 1))
    lane = lax.broadcasted_iota(jnp.int32, (32, 128), 1)
    valid_z = lane < NZ - 1
    for x in range(NX):
        for p in range(2):
            n = x * 2 + p
            t = n * 48
            f = (0.5 * SCALE) * xy[n * 40 : n * 40 + 40, :]
            lower, upper, vb = face(
                f,
                dy[t + 7 : t + 47, :],
                dy[t + 8 : t + 48, :],
                cy[t + 7 : t + 47, :],
                cy[t + 8 : t + 48, :],
                valid_y,
            )
            tly[n * 40 : n * 40 + 40, :] = lower
            vby[n * 40 : n * 40 + 40, :] = vb
            s = p * 512 + x * 32
            f = (0.5 * SCALE) * xe[n * 32 : n * 32 + 32, :]
            dl, cl = d[s : s + 32, :], c[s : s + 32, :]
            du, cu = pltpu.roll(dl, NZ - 1, 1), pltpu.roll(cl, NZ - 1, 1)
            lower_z, upper_z, vb_z = face(f, dl, du, cl, cu, valid_z)
            wz[n * 32 : n * 32 + 32, :] = vb_z
            base[s : s + 32, :] = (
                base[s : s + 32, :] + upper[0:32, :] + (lower_z + pltpu.roll(upper_z, 1, 1))
            )
    for x in range(NX):
        for p in range(2):
            n = x * 2 + p
            s = p * 512 + x * 32
            base[s : s + 32, :] = base[s : s + 32, :] + tly[n * 40 + 1 : n * 40 + 33, :]
            wy[n * 32 : n * 32 + 32, :] = vby[n * 40 : n * 40 + 32, :] + vby[n * 40 + 1 : n * 40 + 33, :]

    for r in range(0, 1024, 64):
        wx[r : r + 64, :] = dot_rows(wx[r : r + 64, :], mze)
        wy[r : r + 64, :] = dot_rows(wy[r : r + 64, :], mze)
        wz[r : r + 64, :] = dot_rows(wz[r : r + 64, :], mzot)

    zero = jnp.zeros((64, 128), f32)

    def at(ref, plane):
        if 0 <= plane < NX:
            return ref[plane * 64 : plane * 64 + 64, :]
        return zero

    bx, t, bz, by = zero, zero, zero, zero
    for m in range(-9, 23):
        new, old = at(wx, m + 9), at(wx, m - 8)
        t = t + (8.0 * (new + old) + (old - bx))
        bx = bx + (new - old)
        bz = bz + (at(wz, m + 9) - at(wz, m - 8))
        by = by + (at(wy, m + 9) - at(wy, m - 8))
        q = (m + 9) * 64
        s1[q : q + 64, :] = bz - 2.0 * t
        s2[q : q + 64, :] = by

    def at2(ref, i):
        if 0 <= i < 32:
            return ref[i * 64 : i * 64 + 64, :]
        return zero

    matt = myt[...]
    ge, go = zero, zero
    for k in range(48):
        ge = ge + (at2(s1, k) - at2(s1, k - 17))
        go = go + (at2(s2, k) - at2(s2, k - 17))
        both = jnp.concatenate(
            [jnp.concatenate([ge[r : r + 32], go[r : r + 32]], 0) for r in (0, 32)], 1
        )
        hi, lo = split(both)
        out = dot(matt, jnp.concatenate([hi, lo], 0))
        for p in range(2):
            z = slice(p * 128, p * 128 + 128)
            if 16 <= k < 32:
                n = (k - 16) * 2 + p
                low[n * 16 : n * 16 + 16, :] = out[0:16, z]
                own[n * 32 : n * 32 + 32, :] = out[16:48, z]
                high[n * 16 : n * 16 + 16, :] = out[48:64, z]
            else:
                n = (k if k < 16 else k - 16) * 2 + p
                hm[n * 32 : n * 32 + 16, :] = out[0:16, z]
                gm[n * 32 : n * 32 + 32, :] = out[16:48, z]
                hm[n * 32 + 16 : n * 32 + 32, :] = out[48:64, z]
    to_a = pl.ds(pl.multiple_of((1 - odd_core) * 1024, 1024), 1024)
    to_b = pl.ds(pl.multiple_of(odd_core * 1024, 1024), 1024)
    ha[...] = hm[to_a, :]
    hb[...] = hm[to_b, :]
    ga[...] = gm[to_a, :]
    gb[...] = gm[to_b, :]


def margin_kernel(low, high, ha, hb, dn, up):
    for n in range(32):
        r, q = n * 16, n * 32
        dn[r : r + 16, :] = low[r : r + 16, :] + (ha[q : q + 16, :] + hb[q : q + 16, :])
        up[r : r + 16, :] = high[r : r + 16, :] + (ha[q + 16 : q + 32, :] + hb[q + 16 : q + 32, :])


def final_kernel(adh, base, own, ga, gb, yl, yr, out):
    h = 0.5 * SCALE
    for x in range(NX):
        pb = []
        for p in range(2):
            q = x * 32 + p * 16
            r = 2 * q
            got = jnp.concatenate([yl[q : q + 16, :], yr[q : q + 16, :]], 0)
            pb.append(own[r : r + 32, :] + (ga[r : r + 32, :] + gb[r : r + 32, :]) + got)
        for p in range(2):
            s = p * 512 + x * 32
            out[s : s + 32, :] = base[s : s + 32, :] + (
                (h * adh[0, p]) * pb[0] + (h * adh[1, p]) * pb[1]
            )


def rows(n):
    return jax.ShapeDtypeStruct((n, 128), f32)


def scratch(n):
    return pltpu.VMEM((n, 128), f32)


def call(kernel, smem, args, out_rows, scratch_rows=()):
    spec = pl.BlockSpec(memory_space=pltpu.VMEM)
    in_rows = sum(a.shape[0] for a in args[smem:])
    total = in_rows + sum(out_rows) + sum(scratch_rows)
    outs = [spec] * len(out_rows)
    shapes = [rows(n) for n in out_rows]
    single = len(out_rows) == 1
    return pl.pallas_call(
        kernel,
        out_shape=shapes[0] if single else shapes,
        in_specs=[pl.BlockSpec(memory_space=pltpu.SMEM)] * smem + [spec] * (len(args) - smem),
        out_specs=outs[0] if single else outs,
        scratch_shapes=[scratch(n) for n in scratch_rows],
        compiler_params=pltpu.CompilerParams(vmem_limit_bytes=total * 512 + (2 << 20)),
    )(*args)


def shift(values, axis, by):
    n = lax.axis_size(axis)
    pairs = [(i, i + by) for i in range(n) if 0 <= i + by < n]
    return lax.ppermute(values, axis, pairs)


def swap(values, first):
    n = lax.axis_size("gx")
    pairs = []
    for i in range(first, n - 1, 2):
        pairs += [(i, i + 1), (i + 1, i)]
    return lax.ppermute(values, "gx", pairs)


def step(density, cotangent, adhesion):
    gx, gy = lax.axis_index("gx"), lax.axis_index("gy")
    nx, ny = lax.axis_size("gx"), lax.axis_size("gy")
    info = jnp.stack([gx % 2, gx > 0, gx < nx - 1, gy > 0, gy < ny - 1]).astype(jnp.int32)
    smem = pl.BlockSpec(memory_space=pltpu.SMEM)
    info, adhesion = pl.pallas_call(
        scalars_kernel,
        out_shape=[
            jax.ShapeDtypeStruct((5,), jnp.int32),
            jax.ShapeDtypeStruct((2, 2), f32),
        ],
        in_specs=[smem, smem],
        out_specs=[smem, smem],
        compiler_params=pltpu.CompilerParams(vmem_limit_bytes=1 << 20),
    )(info, adhesion)
    my = jnp.asarray(y_matrix(), bf16)
    myt = jnp.asarray(y_transposed(), bf16)
    ze, zo, zot = (jnp.asarray(m, bf16) for m in z_matrices())
    d = density.reshape(1024, 128)
    c = cotangent.reshape(1024, 128)

    up, dn = call(pack_kernel, 0, [d, c], [YROWS, YROWS])
    yl = shift(up, "gy", 1)
    yr = shift(dn, "gy", -1)
    bb = swap(d, 1)
    ba = swap(d, 0)
    ma, mb, e0, e15 = call(
        corner_kernel, 1, [info, d, c, yl, yr], [CROWS, CROWS, 128, 128]
    )
    kb = swap(mb, 1)
    ka = swap(ma, 0)
    r2l = shift(e15, "gx", 2)
    r2r = shift(e0, "gx", -2)
    base, own, low, high, ga, gb, ha, hb = call(
        main_kernel,
        2,
        [info, adhesion, d, c, yl, yr, ba, bb, ka, kb, r2l, r2r, my, ze, zo, zot, myt],
        [1024, 1024, 512, 512, 1024, 1024, 1024, 1024],
        [
            50 * 64, 48 * 80, 32 * 80, 34 * 64, 17 * 64, 16 * 64, 16 * 80,
            32 * 48, 32 * 48, 32 * 40, 32 * 40, 1024, 1024, 1024, 256, 1536, 2048, 2048,
        ],
    )
    hb2 = swap(hb, 1)
    ha2 = swap(ha, 0)
    gb2 = swap(gb, 1)
    ga2 = swap(ga, 0)
    dn2, up2 = call(margin_kernel, 0, [low, high, ha2, hb2], [512, 512])
    yl2 = shift(up2, "gy", 1)
    yr2 = shift(dn2, "gy", -1)
    out = call(final_kernel, 1, [adhesion, base, own, ga2, gb2, yl2, yr2], [1024])
    return out.reshape(density.shape)


def solution(mesh):
    return jax.shard_map(
        step,
        mesh=mesh,
        in_specs=(P(None, "gx", "gy", None), P(None, "gx", "gy", None), P()),
        out_specs=P(None, "gx", "gy", None),
        check_vma=False,
    )
```

time: 145 us -> 82.2 us (0.57)
  the two profiles are of different devices: /device:TPU:103 before, /device:TPU:111 now
where the time goes in v1:
time: 82.2 us; the launch traced here: 81.7 us
  starting transfers between devices  40.4 us (49%)
  waiting for transfers between devices  28.8 us (35%)
  Pallas kernels  9.44 us (11%)
  local copies, waits for them, and re-layouts  2.79 us (3%)
    ppermute x6, waiting for transfers between devices, shift(): return lax.ppermute(values, axis, pairs)  25.5 us
    ppermute x8, starting transfers between devices, swap(): return lax.ppermute(values, 'gx', pairs)  23 us
    ppermute x6, starting transfers between devices, shift(): return lax.ppermute(values, axis, pairs)  17.4 us
    pallas_call x5, Pallas kernels, call(): pl.pallas_call(kernel, out_shape=shapes[0] if single else shapes, in_spec...  8.28 us
    ppermute x8, waiting for transfers between devices, swap(): return lax.ppermute(values, 'gx', pairs)  3.26 us
    unnamed x20, local copies, waits for them, and re-layouts  2.71 us
  transfers between devices with their start and end apart: 14, of which 8 were waited for; matrix products, arithmetic and copies ran while one was open for 0% of the time, Pallas kernels for 2%

profile of v1, /device:TPU:111, one launch (start us, length us, event | category | flops | bytes accessed | tf_op | source)
XLA Modules:
  0.0 81.7 jit_solution(16516823880134725041)
XLA Ops:
  0.0 1.0 %copy-done = f32[2,16,32,128]{3,2,1,0:T(8,128)S(1)} copy-done((f32[2,16,32,128]{3,2,1,0:T(8,128)S(1)}, f32[2,16,32,128]{3,2,1,0:T(8,128)}, u32[]{:S(2)}) %copy-start) | copy-done | bytes 524312
  1.0 1.0 %copy-done.2 = f32[2,16,32,128]{3,2,1,0:T(8,128)S(1)} copy-done((f32[2,16,32,128]{3,2,1,0:T(8,128)S(1)}, f32[2,16,32,128]{3,2,1,0:T(8,128)}, u32[]{:S(2)}) %copy-start.2) | copy-done | bytes 524312
  2.1 0.1 shard_map.83
  2.2 3.3 %collective-permute-start = (f32[576,128]{1,0:T(8,128)S(1)}, f32[576,128]{1,0:T(8,128)S(1)}, u32[]{:S(2)}, u32[]{:S(2)}) collective-permute-start(f32[576,128]{1,0:T(8,128)S(1)} %get-tuple-element.25), channel_id=1, source_target_pairs={{0,1},{1,2},{2,3},{3,4},{4,5},{5,6},{6,7},{7,8},{8,9},{9,10},{10,1... | collective-permute-start | bytes 884744 | tf_op jit(solution)/shard_map/ppermute | solution.py:431
  5.4 2.2 %collective-permute-start.1 = (f32[576,128]{1,0:T(8,128)S(1)}, f32[576,128]{1,0:T(8,128)S(1)}, u32[]{:S(2)}, u32[]{:S(2)}) collective-permute-start(f32[576,128]{1,0:T(8,128)S(1)} %get-tuple-element.26), channel_id=1, source_target_pairs={{1,0},{2,1},{3,2},{4,3},{5,4},{6,5},{7,6},{8,7},{9,8},{10,9},{11,1... | collective-permute-start | bytes 884744 | tf_op jit(solution)/shard_map/ppermute | solution.py:431
  7.6 0.0 copy-start.9
  7.6 0.1 stack.39.info
  7.7 0.6 copy-done.9
  8.3 1.2 %shard_map.82 = (s32[5]{0:T(128)S(1)}, f32[2,2]{1,0:T(2,128)S(1)}) custom-call(s32[5]{0:T(128)S(1)} %stack.39.info, f32[2,2]{1,0:T(2,128)S(1)} %copy-done.9), custom_call_target="tpu_custom_call" | custom-call | tf_op jit(solution)/shard_map/pallas_call | solution.py:447
  9.5 2.6 %collective-permute-done.yl = f32[576,128]{1,0:T(8,128)S(1)} collective-permute-done((f32[576,128]{1,0:T(8,128)S(1)}, f32[576,128]{1,0:T(8,128)S(1)}, u32[]{:S(2)}, u32[]{:S(2)}) %collective-permute-start) | collective-permute-done | bytes 294944 | tf_op jit(solution)/shard_map/ppermute | solution.py:431
  12.1 5.0 %collective-permute-done.1.yr = f32[576,128]{1,0:T(8,128)S(1)} collective-permute-done((f32[576,128]{1,0:T(8,128)S(1)}, f32[576,128]{1,0:T(8,128)S(1)}, u32[]{:S(2)}, u32[]{:S(2)}) %collective-permute-start.1) | collective-permute-done | bytes 294944 | tf_op jit(solution)/shard_map/ppermute | solution.py:431
  17.0 0.0 copy-done.1
  17.0 0.0 copy-done.3
  17.1 0.0 copy-start.6
  17.1 0.0 copy-start.7
  17.1 0.0 copy-start.8
  17.1 0.6 shard_map.84
  17.7 3.7 %collective-permute-start.4 = (f32[1152,128]{1,0:T(8,128)S(1)}, f32[1152,128]{1,0:T(8,128)S(1)}, u32[]{:S(2)}, u32[]{:S(2)}) collective-permute-start(f32[1152,128]{1,0:T(8,128)S(1)} %get-tuple-element.27), channel_id=1, source_target_pairs={{0,16},{16,0},{32,48},{48,32},{64,80},{80,64},{96,112},{112,96},{1... | collective-permute-start | bytes 1769480 | tf_op jit(solution)/shard_map/ppermute | solution.py:439
  21.5 4.7 %collective-permute-start.5 = (f32[1152,128]{1,0:T(8,128)S(1)}, f32[1152,128]{1,0:T(8,128)S(1)}, u32[]{:S(2)}, u32[]{:S(2)}) collective-permute-start(f32[1152,128]{1,0:T(8,128)S(1)} %get-tuple-element.28), channel_id=1, source_target_pairs={{16,32},{32,16},{48,64},{64,48},{80,96},{96,80},{112,128},{128,112... | collective-permute-start | bytes 1769480 | tf_op jit(solution)/shard_map/ppermute | solution.py:439
  26.1 2.1 %collective-permute-start.3 = (f32[1024,128]{1,0:T(8,128)S(1)}, f32[1024,128]{1,0:T(8,128)S(1)}, u32[]{:S(2)}, u32[]{:S(2)}) collective-permute-start(f32[1024,128]{1,0:T(8,128)S(1)} %bitcast.10), channel_id=1, source_target_pairs={{16,32},{32,16},{48,64},{64,48},{80,96},{96,80},{112,128},{128,112... | collective-permute-start | bytes 1572872 | tf_op jit(solution)/shard_map/ppermute | solution.py:439
  28.2 1.9 %collective-permute-start.2 = (f32[1024,128]{1,0:T(8,128)S(1)}, f32[1024,128]{1,0:T(8,128)S(1)}, u32[]{:S(2)}, u32[]{:S(2)}) collective-permute-start(f32[1024,128]{1,0:T(8,128)S(1)} %bitcast.11), channel_id=1, source_target_pairs={{0,16},{16,0},{32,48},{48,32},{64,80},{80,64},{96,112},{112,96},{1... | collective-permute-start | bytes 1572872 | tf_op jit(solution)/shard_map/ppermute | solution.py:439
  30.2 4.8 %collective-permute-start.6 = (f32[128,128]{1,0:T(8,128)S(1)}, f32[128,128]{1,0:T(8,128)S(1)}, u32[]{:S(2)}, u32[]{:S(2)}) collective-permute-start(f32[128,128]{1,0:T(8,128)S(1)} %get-tuple-element.29), channel_id=1, source_target_pairs={{0,32},{16,48},{32,64},{48,80},{64,96},{80,112},{96,128},{112,144}... | collective-permute-start | bytes 196616 | tf_op jit(solution)/shard_map/ppermute | solution.py:431
  34.9 5.0 %collective-permute-done.6.r2l = f32[128,128]{1,0:T(8,128)S(1)} collective-permute-done((f32[128,128]{1,0:T(8,128)S(1)}, f32[128,128]{1,0:T(8,128)S(1)}, u32[]{:S(2)}, u32[]{:S(2)}) %collective-permute-start.6) | collective-permute-done | bytes 65568 | tf_op jit(solution)/shard_map/ppermute | solution.py:431
  39.9 1.9 %collective-permute-start.7 = (f32[128,128]{1,0:T(8,128)S(1)}, f32[128,128]{1,0:T(8,128)S(1)}, u32[]{:S(2)}, u32[]{:S(2)}) collective-permute-start(f32[128,128]{1,0:T(8,128)S(1)} %get-tuple-element.30), channel_id=1, source_target_pairs={{32,0},{48,16},{64,32},{80,48},{96,64},{112,80},{128,96},{144,112}... | collective-permute-start | bytes 196616 | tf_op jit(solution)/shard_map/ppermute | solution.py:431
  41.9 4.7 %collective-permute-done.7.r2r = f32[128,128]{1,0:T(8,128)S(1)} collective-permute-done((f32[128,128]{1,0:T(8,128)S(1)}, f32[128,128]{1,0:T(8,128)S(1)}, u32[]{:S(2)}, u32[]{:S(2)}) %collective-permute-start.7) | collective-permute-done | bytes 65568 | tf_op jit(solution)/shard_map/ppermute | solution.py:431
  46.6 0.0 collective-permute-done.3.bb
  46.6 0.0 collective-permute-done.2.ba
  46.6 0.0 collective-permute-done.4.ka
  46.6 0.0 collective-permute-done.5.kb
  46.6 0.0 copy-done.4
  46.6 0.0 copy-done.5
  46.7 0.0 copy-done.6
  46.7 0.0 copy-done.7
  46.7 5.9 %shard_map.85 = (f32[1024,128]{1,0:T(8,128)S(1)}, f32[1024,128]{1,0:T(8,128)S(1)}, f32[512,128]{1,0:T(8,128)S(1)}, f32[512,128]{1,0:T(8,128)S(1)}, f32[1024,128]...) custom-call(s32[5]{0:T(128)S(1)} %get-tuple-element.24.info, ...), custom_call_target="tpu_custom_call" | custom-call | tf_op jit(solution)/shard_map/pallas_call | solution.py:418
  52.6 1.9 %collective-permute-start.10 = (f32[1024,128]{1,0:T(8,128)S(1)}, f32[1024,128]{1,0:T(8,128)S(1)}, u32[]{:S(2)}, u32[]{:S(2)}) collective-permute-start(f32[1024,128]{1,0:T(8,128)S(1)} %get-tuple-element.37), channel_id=1, source_target_pairs={{0,16},{16,0},{32,48},{48,32},{64,80},{80,64},{96,112},{112,96},{1... | collective-permute-start | bytes 1572872 | tf_op jit(solution)/shard_map/ppermute | solution.py:439
  54.6 3.7 %collective-permute-start.11 = (f32[1024,128]{1,0:T(8,128)S(1)}, f32[1024,128]{1,0:T(8,128)S(1)}, u32[]{:S(2)}, u32[]{:S(2)}) collective-permute-start(f32[1024,128]{1,0:T(8,128)S(1)} %get-tuple-element.38), channel_id=1, source_target_pairs={{16,32},{32,16},{48,64},{64,48},{80,96},{96,80},{112,128},{128,112... | collective-permute-start | bytes 1572872 | tf_op jit(solution)/shard_map/ppermute | solution.py:439
  58.3 1.9 %collective-permute-start.8 = (f32[1024,128]{1,0:T(8,128)S(1)}, f32[1024,128]{1,0:T(8,128)S(1)}, u32[]{:S(2)}, u32[]{:S(2)}) collective-permute-start(f32[1024,128]{1,0:T(8,128)S(1)} %get-tuple-element.33), channel_id=1, source_target_pairs={{0,16},{16,0},{32,48},{48,32},{64,80},{80,64},{96,112},{112,96},{1... | collective-permute-start | bytes 1572872 | tf_op jit(solution)/shard_map/ppermute | solution.py:439
  60.2 3.0 %collective-permute-start.9 = (f32[1024,128]{1,0:T(8,128)S(1)}, f32[1024,128]{1,0:T(8,128)S(1)}, u32[]{:S(2)}, u32[]{:S(2)}) collective-permute-start(f32[1024,128]{1,0:T(8,128)S(1)} %get-tuple-element.34), channel_id=1, source_target_pairs={{16,32},{32,16},{48,64},{64,48},{80,96},{96,80},{112,128},{128,112... | collective-permute-start | bytes 1572872 | tf_op jit(solution)/shard_map/ppermute | solution.py:439
  63.3 0.0 collective-permute-done.10.ha
  63.3 3.0 %collective-permute-done.11.hb = f32[1024,128]{1,0:T(8,128)S(1)} collective-permute-done((f32[1024,128]{1,0:T(8,128)S(1)}, f32[1024,128]{1,0:T(8,128)S(1)}, u32[]{:S(2)}, u32[]{:S(2)}) %collective-permute-start.11) | collective-permute-done | bytes 524320 | tf_op jit(solution)/shard_map/ppermute | solution.py:439
  66.3 0.1 shard_map.86
  66.4 1.9 %collective-permute-start.12 = (f32[512,128]{1,0:T(8,128)S(1)}, f32[512,128]{1,0:T(8,128)S(1)}, u32[]{:S(2)}, u32[]{:S(2)}) collective-permute-start(f32[512,128]{1,0:T(8,128)S(1)} %get-tuple-element.39), channel_id=1, source_target_pairs={{0,1},{1,2},{2,3},{3,4},{4,5},{5,6},{6,7},{7,8},{8,9},{9,10},{10,1... | collective-permute-start | bytes 786440 | tf_op jit(solution)/shard_map/ppermute | solution.py:431
  68.3 3.4 %collective-permute-start.13 = (f32[512,128]{1,0:T(8,128)S(1)}, f32[512,128]{1,0:T(8,128)S(1)}, u32[]{:S(2)}, u32[]{:S(2)}) collective-permute-start(f32[512,128]{1,0:T(8,128)S(1)} %get-tuple-element.40), channel_id=1, source_target_pairs={{1,0},{2,1},{3,2},{4,3},{5,4},{6,5},{7,6},{8,7},{9,8},{10,9},{11,1... | collective-permute-start | bytes 786440 | tf_op jit(solution)/shard_map/ppermute | solution.py:431
  71.7 0.0 collective-permute-done.8.ga
  71.7 0.3 collective-permute-done.9.gb
  72.0 4.4 %collective-permute-done.12.yl = f32[512,128]{1,0:T(8,128)S(1)} collective-permute-done((f32[512,128]{1,0:T(8,128)S(1)}, f32[512,128]{1,0:T(8,128)S(1)}, u32[]{:S(2)}, u32[]{:S(2)}) %collective-permute-start.12) | collective-permute-done | bytes 262176 | tf_op jit(solution)/shard_map/ppermute | solution.py:431
  76.4 3.8 %collective-permute-done.13.yr = f32[512,128]{1,0:T(8,128)S(1)} collective-permute-done((f32[512,128]{1,0:T(8,128)S(1)}, f32[512,128]{1,0:T(8,128)S(1)}, u32[]{:S(2)}, u32[]{:S(2)}) %collective-permute-start.13) | collective-permute-done | bytes 262176 | tf_op jit(solution)/shard_map/ppermute | solution.py:431
  80.1 1.5 %shard_map.87 = f32[1024,128]{1,0:T(8,128)} custom-call(f32[2,2]{1,0:T(2,128)S(1)} %get-tuple-element.23.adh, f32[1024,128]{1,0:T(8,128)S(1)} %get-tuple-element.31.base, f32[1024,128]{1,0:T(8,128)S(1)} %get-tuple-element.32.own, f32[1024,128]{1,0:T(8,128)S(1)} %collective-permute-done.8.ga, f32[1024,128]{1,0:T(8,128)S(1)} %collective-permute-done.9.gb, ...), custom_call_target="tpu_custom_call" | custom-call | tf_op jit(solution)/shard_map/pallas_call | solution.py:418
  (7 shorter events, 0.0 us)
Async XLA Ops:
  0.0 1.0 %copy-start = (f32[2,16,32,128]{3,2,1,0:T(8,128)S(1)}, f32[2,16,32,128]{3,2,1,0:T(8,128)}, u32[]{:S(2)}) copy-start(f32[2,16,32,128]{3,2,1,0:T(8,128)} %param.8) | copy-start | bytes 1572868
  1.0 1.0 %copy-start.2 = (f32[2,16,32,128]{3,2,1,0:T(8,128)S(1)}, f32[2,16,32,128]{3,2,1,0:T(8,128)}, u32[]{:S(2)}) copy-start(f32[2,16,32,128]{3,2,1,0:T(8,128)} %param.9) | copy-start | bytes 1572868
  2.1 15.0 %copy-start.1 = (f32[2,16,32,128]{3,2,1,0:T(8,128)S(1)}, f32[2,16,32,128]{3,2,1,0:T(8,128)}, u32[]{:S(2)}) copy-start(f32[2,16,32,128]{3,2,1,0:T(8,128)} %param.8) | copy-start | bytes 1572868
  2.1 15.0 %copy-start.3 = (f32[2,16,32,128]{3,2,1,0:T(8,128)S(1)}, f32[2,16,32,128]{3,2,1,0:T(8,128)}, u32[]{:S(2)}) copy-start(f32[2,16,32,128]{3,2,1,0:T(8,128)} %param.9) | copy-start | bytes 1572868
  2.2 9.9 %collective-permute-start = (f32[576,128]{1,0:T(8,128)S(1)}, f32[576,128]{1,0:T(8,128)S(1)}, u32[]{:S(2)}, u32[]{:S(2)}) collective-permute-start(f32[576,128]{1,0:T(8,128)S(1)} %get-tuple-element.25), channel_id=1, source_target_pairs={{0,1},{1,2},{2,3},{3,4},{4,5},{5,6},{6,7},{7,8},{8,9},{9,10},{10,1... | collective-permute-start | bytes 884744 | tf_op jit(solution)/shard_map/ppermute | solution.py:431
  5.4 11.6 %collective-permute-start.1 = (f32[576,128]{1,0:T(8,128)S(1)}, f32[576,128]{1,0:T(8,128)S(1)}, u32[]{:S(2)}, u32[]{:S(2)}) collective-permute-start(f32[576,128]{1,0:T(8,128)S(1)} %get-tuple-element.26), channel_id=1, source_target_pairs={{1,0},{2,1},{3,2},{4,3},{5,4},{6,5},{7,6},{8,7},{9,8},{10,9},{11,1... | collective-permute-start | bytes 884744 | tf_op jit(solution)/shard_map/ppermute | solution.py:431
  7.6 0.7 copy-start.9
  17.0 29.6 %copy-start.4 = (bf16[256,128]{1,0:T(8,128)(2,1)S(1)}, bf16[256,128]{1,0:T(8,128)(2,1)}, u32[]{:S(2)}) copy-start(bf16[256,128]{1,0:T(8,128)(2,1)} %constant.41.clone.zot) | copy-start | bytes 196612
  17.1 29.6 %copy-start.5 = (bf16[256,128]{1,0:T(8,128)(2,1)S(1)}, bf16[256,128]{1,0:T(8,128)(2,1)}, u32[]{:S(2)}) copy-start(bf16[256,128]{1,0:T(8,128)(2,1)} %constant.40.clone.zo) | copy-start | bytes 196612
  17.1 29.6 %copy-start.6 = (bf16[256,128]{1,0:T(8,128)(2,1)S(1)}, bf16[256,128]{1,0:T(8,128)(2,1)}, u32[]{:S(2)}) copy-start(bf16[256,128]{1,0:T(8,128)(2,1)} %constant.39.clone.ze) | copy-start | bytes 196612
  17.1 29.6 %copy-start.7 = (bf16[80,160]{1,0:T(8,128)(2,1)S(1)}, bf16[80,160]{1,0:T(8,128)(2,1)}, u32[]{:S(2)}) copy-start(bf16[80,160]{1,0:T(8,128)(2,1)} %constant.37.clone.my) | copy-start | bytes 76804
  17.1 29.6 %copy-start.8 = (bf16[64,128]{1,0:T(8,128)(2,1)S(1)}, bf16[64,128]{1,0:T(8,128)(2,1)}, u32[]{:S(2)}) copy-start(bf16[64,128]{1,0:T(8,128)(2,1)} %constant.38.clone.myt) | copy-start | bytes 49156
  17.7 28.9 %collective-permute-start.4 = (f32[1152,128]{1,0:T(8,128)S(1)}, f32[1152,128]{1,0:T(8,128)S(1)}, u32[]{:S(2)}, u32[]{:S(2)}) collective-permute-start(f32[1152,128]{1,0:T(8,128)S(1)} %get-tuple-element.27), channel_id=1, source_target_pairs={{0,16},{16,0},{32,48},{48,32},{64,80},{80,64},{96,112},{112,96},{1... | collective-permute-start | bytes 1769480 | tf_op jit(solution)/shard_map/ppermute | solution.py:439
  21.5 25.2 %collective-permute-start.5 = (f32[1152,128]{1,0:T(8,128)S(1)}, f32[1152,128]{1,0:T(8,128)S(1)}, u32[]{:S(2)}, u32[]{:S(2)}) collective-permute-start(f32[1152,128]{1,0:T(8,128)S(1)} %get-tuple-element.28), channel_id=1, source_target_pairs={{16,32},{32,16},{48,64},{64,48},{80,96},{96,80},{112,128},{128,112... | collective-permute-start | bytes 1769480 | tf_op jit(solution)/shard_map/ppermute | solution.py:439
  26.1 20.5 %collective-permute-start.3 = (f32[1024,128]{1,0:T(8,128)S(1)}, f32[1024,128]{1,0:T(8,128)S(1)}, u32[]{:S(2)}, u32[]{:S(2)}) collective-permute-start(f32[1024,128]{1,0:T(8,128)S(1)} %bitcast.10), channel_id=1, source_target_pairs={{16,32},{32,16},{48,64},{64,48},{80,96},{96,80},{112,128},{128,112... | collective-permute-start | bytes 1572872 | tf_op jit(solution)/shard_map/ppermute | solution.py:439
  28.2 18.4 %collective-permute-start.2 = (f32[1024,128]{1,0:T(8,128)S(1)}, f32[1024,128]{1,0:T(8,128)S(1)}, u32[]{:S(2)}, u32[]{:S(2)}) collective-permute-start(f32[1024,128]{1,0:T(8,128)S(1)} %bitcast.11), channel_id=1, source_target_pairs={{0,16},{16,0},{32,48},{48,32},{64,80},{80,64},{96,112},{112,96},{1... | collective-permute-start | bytes 1572872 | tf_op jit(solution)/shard_map/ppermute | solution.py:439
  30.2 9.8 %collective-permute-start.6 = (f32[128,128]{1,0:T(8,128)S(1)}, f32[128,128]{1,0:T(8,128)S(1)}, u32[]{:S(2)}, u32[]{:S(2)}) collective-permute-start(f32[128,128]{1,0:T(8,128)S(1)} %get-tuple-element.29), channel_id=1, source_target_pairs={{0,32},{16,48},{32,64},{48,80},{64,96},{80,112},{96,128},{112,144}... | collective-permute-start | bytes 196616 | tf_op jit(solution)/shard_map/ppermute | solution.py:431
  39.9 6.7 %collective-permute-start.7 = (f32[128,128]{1,0:T(8,128)S(1)}, f32[128,128]{1,0:T(8,128)S(1)}, u32[]{:S(2)}, u32[]{:S(2)}) collective-permute-start(f32[128,128]{1,0:T(8,128)S(1)} %get-tuple-element.30), channel_id=1, source_target_pairs={{32,0},{48,16},{64,32},{80,48},{96,64},{112,80},{128,96},{144,112}... | collective-permute-start | bytes 196616 | tf_op jit(solution)/shard_map/ppermute | solution.py:431
  52.6 10.6 %collective-permute-start.10 = (f32[1024,128]{1,0:T(8,128)S(1)}, f32[1024,128]{1,0:T(8,128)S(1)}, u32[]{:S(2)}, u32[]{:S(2)}) collective-permute-start(f32[1024,128]{1,0:T(8,128)S(1)} %get-tuple-element.37), channel_id=1, source_target_pairs={{0,16},{16,0},{32,48},{48,32},{64,80},{80,64},{96,112},{112,96},{1... | collective-permute-start | bytes 1572872 | tf_op jit(solution)/shard_map/ppermute | solution.py:439
  54.6 11.7 %collective-permute-start.11 = (f32[1024,128]{1,0:T(8,128)S(1)}, f32[1024,128]{1,0:T(8,128)S(1)}, u32[]{:S(2)}, u32[]{:S(2)}) collective-permute-start(f32[1024,128]{1,0:T(8,128)S(1)} %get-tuple-element.38), channel_id=1, source_target_pairs={{16,32},{32,16},{48,64},{64,48},{80,96},{96,80},{112,128},{128,112... | collective-permute-start | bytes 1572872 | tf_op jit(solution)/shard_map/ppermute | solution.py:439
  58.3 13.4 %collective-permute-start.8 = (f32[1024,128]{1,0:T(8,128)S(1)}, f32[1024,128]{1,0:T(8,128)S(1)}, u32[]{:S(2)}, u32[]{:S(2)}) collective-permute-start(f32[1024,128]{1,0:T(8,128)S(1)} %get-tuple-element.33), channel_id=1, source_target_pairs={{0,16},{16,0},{32,48},{48,32},{64,80},{80,64},{96,112},{112,96},{1... | collective-permute-start | bytes 1572872 | tf_op jit(solution)/shard_map/ppermute | solution.py:439
  60.2 11.7 %collective-permute-start.9 = (f32[1024,128]{1,0:T(8,128)S(1)}, f32[1024,128]{1,0:T(8,128)S(1)}, u32[]{:S(2)}, u32[]{:S(2)}) collective-permute-start(f32[1024,128]{1,0:T(8,128)S(1)} %get-tuple-element.34), channel_id=1, source_target_pairs={{16,32},{32,16},{48,64},{64,48},{80,96},{96,80},{112,128},{128,112... | collective-permute-start | bytes 1572872 | tf_op jit(solution)/shard_map/ppermute | solution.py:439
  66.4 10.0 %collective-permute-start.12 = (f32[512,128]{1,0:T(8,128)S(1)}, f32[512,128]{1,0:T(8,128)S(1)}, u32[]{:S(2)}, u32[]{:S(2)}) collective-permute-start(f32[512,128]{1,0:T(8,128)S(1)} %get-tuple-element.39), channel_id=1, source_target_pairs={{0,1},{1,2},{2,3},{3,4},{4,5},{5,6},{6,7},{7,8},{8,9},{9,10},{10,1... | collective-permute-start | bytes 786440 | tf_op jit(solution)/shard_map/ppermute | solution.py:431
  68.3 11.8 %collective-permute-start.13 = (f32[512,128]{1,0:T(8,128)S(1)}, f32[512,128]{1,0:T(8,128)S(1)}, u32[]{:S(2)}, u32[]{:S(2)}) collective-permute-start(f32[512,128]{1,0:T(8,128)S(1)} %get-tuple-element.40), channel_id=1, source_target_pairs={{1,0},{2,1},{3,2},{4,3},{5,4},{6,5},{7,6},{8,7},{9,8},{10,9},{11,1... | collective-permute-start | bytes 786440 | tf_op jit(solution)/shard_map/ppermute | solution.py:431

commit v2 on v1

v2 whole, which is shorter than its diff:
```python
import jax
import jax.numpy as jnp
import numpy as np
from jax import lax
from jax.experimental import pallas as pl
from jax.experimental.pallas import tpu as pltpu
from jax.sharding import PartitionSpec as P


R = 16
W = R + 1
NX = 16
NY = 32
NZ = 128
f32 = jnp.float32
bf16 = jnp.bfloat16

SMOOTH2 = 0.01
STEP = 0.5

offs = np.arange(-R, R + 1).astype(np.float64)
even_norm = np.sqrt(np.sum((W - np.abs(offs)) ** 2))
odd_norm = np.sqrt(np.sum((offs * (W - np.abs(offs))) ** 2))
SCALE = float(1.0 / (even_norm * even_norm * odd_norm))


def even(d):
    return np.where(np.abs(d) <= R, W - np.abs(d), 0).astype(np.float32)


def odd(d):
    return np.where(np.abs(d) <= R, d * (W - np.abs(d)), 0).astype(np.float32)


def y_matrix():
    lines = np.full(80, 10**6)
    lines[0:64] = np.arange(-16, 48)
    lines[64] = -17
    lines[65] = 48
    m = np.zeros((80, 80), np.float32)
    for c in range(NY):
        m[c] = even(lines - c)
    for j in range(NY + 1):
        m[NY + j] = odd(lines - (j - 1)) + odd(lines - j)
    return np.concatenate([m, m], 1)


def y_transposed():
    k = np.arange(-16, 48)[:, None]
    c = np.arange(NY)[None, :]
    m = np.concatenate([even(k - c), odd(k - c)], 1)
    return np.concatenate([m, m], 1)


def z_matrices():
    k = np.arange(NZ)[:, None]
    j = np.arange(NZ)[None, :]
    ze = even(k - j)
    zo = odd(k - j) + odd(k - j - 1)
    zo[:, NZ - 1] = 0
    return [np.concatenate([m, m], 0) for m in (ze, zo, zo.T)]


def split(x):
    hi = x.astype(bf16)
    lo = (x - hi.astype(f32)).astype(bf16)
    return hi, lo


def dot(a, b):
    return jnp.dot(a, b, preferred_element_type=f32)


def dot_rows(x, m):
    hi, lo = split(x)
    return dot(jnp.concatenate([hi, lo], 1), m)


YROWS = 576
CROWS = 544 * 2 + 64


def spread_kernel(adh, out):
    for i in range(2):
        for j in range(2):
            out[i * 16 + j * 8 : i * 16 + j * 8 + 8, :] = jnp.full((8, 128), adh[i, j], f32)


def adhesion_rows(av):
    return [av[i * 8 : i * 8 + 1, :] for i in range(4)]


def pack_kernel(d, c, up, dn, dv, cv, sems):
    copies = []
    for i, (src, dst) in enumerate(((d, dv), (c, cv))):
        for k in range(4):
            part = pl.ds(k * 256, 256)
            copies.append(pltpu.make_async_copy(src.at[part], dst.at[part], sems.at[i * 4 + k]))
    for copy in copies:
        copy.start()
    for copy in copies[:4]:
        copy.wait()
    for n in range(32):
        up[n * 16 : n * 16 + 16, :] = dv[n * 32 + 16 : n * 32 + 32, :]
        dn[n * 16 : n * 16 + 16, :] = dv[n * 32 : n * 32 + 16, :]
    up[512:544, :] = dv[pl.ds(15, 32, stride=32), :]
    dn[512:544, :] = dv[pl.ds(16, 32, stride=32), :]
    for copy in copies[4:]:
        copy.wait()
    up[544:576, :] = cv[pl.ds(31, 32, stride=32), :]
    dn[544:576, :] = cv[pl.ds(0, 32, stride=32), :]


def corner_kernel(av, d, c, yl, yr, ma, mb, e0, e15):
    edge = lax.rem(lax.axis_index("gx"), 2)
    for ref in (ma, mb):
        ref[0:544, :] = yl[0:544, :]
        ref[544:1088, :] = yr[0:544, :]
    for p in range(2):
        near = pl.multiple_of(p * 512 + (1 - edge) * 480, 32)
        far = pl.multiple_of(p * 512 + edge * 480, 32)
        r = 1088 + p * 32
        ma[r : r + 32, :] = c[pl.ds(near, 32), :]
        mb[r : r + 32, :] = c[pl.ds(far, 32), :]
        for ref, x in ((e0, 0), (e15, NX - 1)):
            n = p * 16 + x
            ref[p * 64 : p * 64 + 16, :] = yl[n * 16 : n * 16 + 16, :]
            ref[p * 64 + 16 : p * 64 + 48, :] = d[n * 32 : n * 32 + 32, :]
            ref[p * 64 + 48 : p * 64 + 64, :] = yr[n * 16 : n * 16 + 16, :]


def face_bar(f, dl, du, cl, cu, valid):
    r = lax.rsqrt(f * f + SMOOTH2)
    fb = (0.5 * STEP) * (cu - cl)
    if valid is not None:
        fb = jnp.where(valid, fb, 0.0)
    return fb * ((dl + du) - (f * r) * (du - dl))


def face_sides(f, cl, cu, valid):
    g = f * f + SMOOTH2
    mag = g * lax.rsqrt(g)
    fb = (0.5 * STEP) * (cu - cl)
    if valid is not None:
        fb = jnp.where(valid, fb, 0.0)
    return fb * (f + mag), fb * (f - mag)


def y_filter(mat, av, parts):
    a00, a01, a10, a11 = adhesion_rows(av)
    both = jnp.concatenate(
        [a00 * parts[0] + a01 * parts[1], a10 * parts[0] + a11 * parts[1]], 1
    )
    hi, lo = split(both)
    return dot(mat, jnp.concatenate([hi, lo], 0))


def y_filter_block(mat, av, blk, kl, ol, kr, oh, ext, store):
    ext[...] = jnp.zeros((512, 128), f32)
    ext[pl.ds(0, 32, stride=16), :] = kl[ol + 512 : ol + 544, :]
    ext[pl.ds(1, 32, stride=16), :] = kr[oh + 512 : oh + 544, :]
    for x in range(NX):
        parts = []
        for p in range(2):
            n = p * 16 + x
            parts.append(
                jnp.concatenate(
                    [
                        kl[ol + n * 16 : ol + n * 16 + 16, :],
                        blk[n * 32 : n * 32 + 32, :],
                        kr[oh + n * 16 : oh + n * 16 + 16, :],
                        ext[n * 16 : n * 16 + 16, :],
                    ],
                    0,
                )
            )
        out = y_filter(mat, av, parts)
        for p in range(2):
            z = slice(p * 128, p * 128 + 128)
            store(x, p, out[0:32, z], out[32:72, z])


def y_own_kernel(av, d, yl, yr, my, seo, soo, ext):
    def store(x, p, e, o):
        n = x * 2 + p
        seo[n * 32 : n * 32 + 32, :] = e
        soo[n * 40 : n * 40 + 40, :] = o

    y_filter_block(my[...], av, d, yl, 0, yr, 0, ext, store)


def masks(axis):
    i, n = lax.axis_index(axis), lax.axis_size(axis)
    return i > 0, i < n - 1


def y_mask():
    below, above = masks("gy")
    row = lax.broadcasted_iota(jnp.int32, (40, 128), 0)
    first = jnp.where(below, 0, 1)
    last = jnp.where(above, 32, 31)
    return (row >= first) & (row <= last)


def z_mask():
    return lax.broadcasted_iota(jnp.int32, (32, 128), 1) < NZ - 1


def x_face_cells(edges, d, p, j, base):
    lo, hi = p * 512 + (j - 1) * 32, p * 512 + j * 32
    low = edges[base + p * 32 : base + p * 32 + 32, :] if j == 0 else d[lo : lo + 32, :]
    r = 128 + base + p * 32
    high = edges[r : r + 32, :] if j == 16 else d[hi : hi + 32, :]
    return low, high


def main_kernel(
    av, d, c, yl, yr, ba, bb, ka, kb, r2l, r2r, seo, soo, my, ze, zo, zot, myt,
    own, low, high, am, gb, hb, xo, xe, xy, dy, cy, edges,
    se, so, s1, s2, vby, wx, wy, wz, ext, gm, hm,
):
    odd_core = lax.rem(lax.axis_index("gx"), 2)
    left, right = masks("gx")

    mat = my[...]
    for blk, k, side in ((ba, ka, 1 - odd_core), (bb, kb, odd_core)):

        def store(x, p, e, o, side=side):
            se[pl.ds(pl.multiple_of((16 * side + 1 + x) * 64 + p * 32, 32), 32), :] = e
            so[pl.ds(pl.multiple_of((16 * side + x) * 80 + p * 40, 8), 40), :] = o

        y_filter_block(mat, av, blk, k, 0, k, 544, ext, store)
    for ref, q in ((r2l, 0), (r2r, 33)):
        zero16 = jnp.zeros((16, 128), f32)
        parts = [jnp.concatenate([ref[p * 64 : p * 64 + 64, :], zero16], 0) for p in range(2)]
        out = y_filter(mat, av, parts)
        for p in range(2):
            se[q * 64 + p * 32 : q * 64 + p * 32 + 32, :] = out[0:32, p * 128 : p * 128 + 128]
    for ref, kref, side in ((ba, ka, 1 - odd_core), (bb, kb, odd_core)):
        q = pl.multiple_of(side * 128, 128)
        for p in range(2):
            src = pl.multiple_of(p * 512 + (1 - side) * 480, 32)
            edges[pl.ds(q + p * 32, 32), :] = ref[pl.ds(src, 32), :]
        edges[pl.ds(q + 64, 64), :] = kref[1088:1152, :]

    def pe(plane):
        if 0 <= plane < NX:
            return seo[plane * 64 : plane * 64 + 64, :]
        q = (plane + 17 if plane < 0 else plane + 1) * 64
        return se[q : q + 64, :]

    def po(plane):
        if 0 <= plane < NX:
            return soo[plane * 80 : plane * 80 + 80, :]
        q = (plane + 16 if plane < 0 else plane) * 80
        return so[q : q + 80, :]

    b = pe(-17)
    for k in range(-16, 0):
        b = b + pe(k)
    t = None
    for j in range(1, 9):
        term = float(j) * (pe(-9 + j) - pe(-9 - j))
        t = term if t is None else t + term
    s2[0:64, :] = t
    for m in range(-9, 24):
        new, old = pe(m + 9), pe(m - 8)
        t = t + (8.0 * (new + old) + (old - b))
        s2[(m + 10) * 64 : (m + 11) * 64, :] = t
        if m < 23:
            b = b + (new - old)
            s1[(m + 9) * 64 : (m + 10) * 64, :] = b
    e = s1[0:64, :]
    for m in range(1, 17):
        e = e + s1[m * 64 : m * 64 + 64, :]
    xe[0:64, :] = e
    for k in range(15):
        e = e + (s1[(k + 17) * 64 : (k + 18) * 64, :] - s1[k * 64 : k * 64 + 64, :])
        xe[(k + 1) * 64 : (k + 2) * 64, :] = e
    o = s2[0:64, :]
    for m in range(1, 17):
        o = o + s2[m * 64 : m * 64 + 64, :]
    for j in range(17):
        nxt = o + (s2[(j + 17) * 64 : (j + 18) * 64, :] - s2[j * 64 : j * 64 + 64, :])
        xo[j * 64 : j * 64 + 64, :] = o + nxt
        o = nxt
    b = po(-16)
    for k in range(-15, 1):
        b = b + po(k)
    s1[0:80, :] = b
    for m in range(-8, 23):
        b = b + (po(m + 9) - po(m - 8))
        s1[(m + 9) * 80 : (m + 10) * 80, :] = b
    e = s1[0:80, :]
    for m in range(1, 17):
        e = e + s1[m * 80 : m * 80 + 80, :]
    xy[0:80, :] = e
    for k in range(15):
        e = e + (s1[(k + 17) * 80 : (k + 18) * 80, :] - s1[k * 80 : k * 80 + 80, :])
        xy[(k + 1) * 80 : (k + 2) * 80, :] = e

    mze, mzo, mzot = ze[...], zo[...], zot[...]
    for r in range(0, 1088, 64):
        xo[r : r + 64, :] = dot_rows(xo[r : r + 64, :], mze)
    for r in range(0, 1280, 80):
        xy[r : r + 80, :] = dot_rows(xy[r : r + 80, :], mze)
    for r in range(0, 1024, 64):
        xe[r : r + 64, :] = dot_rows(xe[r : r + 64, :], mzo)

    for p in range(2):
        prev = None
        for j in range(17):
            f = SCALE * xo[j * 64 + p * 32 : j * 64 + p * 32 + 32, :]
            dl, du = x_face_cells(edges, d, p, j, 0)
            cl, cu = x_face_cells(edges, c, p, j, 64)
            vb = face_bar(f, dl, du, cl, cu, {0: left, 16: right}.get(j))
            if j:
                r = (j - 1) * 64 + p * 32
                wx[r : r + 32, :] = vb + prev
            prev = vb

    for p in range(2):
        q = p * 16
        dy[pl.ds(p * 48 + 7, 16, stride=96), :] = yl[pl.ds(p * 256 + 15, 16, stride=16), :]
        dy[pl.ds(p * 48 + 40, 16, stride=96), :] = yr[pl.ds(p * 256, 16, stride=16), :]
        cy[pl.ds(p * 48 + 7, 16, stride=96), :] = yl[544 + q : 560 + q, :]
        cy[pl.ds(p * 48 + 40, 16, stride=96), :] = yr[544 + q : 560 + q, :]
        for x in range(NX):
            s = p * 512 + x * 32
            t = (x * 2 + p) * 48 + 8
            dy[t : t + 32, :] = d[s : s + 32, :]
            cy[t : t + 32, :] = c[s : s + 32, :]
    valid_y, valid_z = y_mask(), z_mask()
    for x in range(NX):
        for p in range(2):
            n = x * 2 + p
            t = n * 48
            f = (0.5 * SCALE) * xy[n * 40 : n * 40 + 40, :]
            vby[n * 40 : n * 40 + 40, :] = face_bar(
                f,
                dy[t + 7 : t + 47, :],
                dy[t + 8 : t + 48, :],
                cy[t + 7 : t + 47, :],
                cy[t + 8 : t + 48, :],
                valid_y,
            )
            s = p * 512 + x * 32
            f = (0.5 * SCALE) * xe[n * 32 : n * 32 + 32, :]
            dl, cl = d[s : s + 32, :], c[s : s + 32, :]
            du, cu = pltpu.roll(dl, NZ - 1, 1), pltpu.roll(cl, NZ - 1, 1)
            wz[n * 32 : n * 32 + 32, :] = face_bar(f, dl, du, cl, cu, valid_z)
    for n in range(32):
        wy[n * 32 : n * 32 + 32, :] = vby[n * 40 : n * 40 + 32, :] + vby[n * 40 + 1 : n * 40 + 33, :]

    for r in range(0, 1024, 64):
        wx[r : r + 64, :] = dot_rows(wx[r : r + 64, :], mze)
        wy[r : r + 64, :] = dot_rows(wy[r : r + 64, :], mze)
        wz[r : r + 64, :] = dot_rows(wz[r : r + 64, :], mzot)

    zero = jnp.zeros((64, 128), f32)

    def at(ref, plane):
        if 0 <= plane < NX:
            return ref[plane * 64 : plane * 64 + 64, :]
        return zero

    bx, t, bz, by = zero, zero, zero, zero
    for m in range(-9, 23):
        new, old = at(wx, m + 9), at(wx, m - 8)
        t = t + (8.0 * (new + old) + (old - bx))
        bx = bx + (new - old)
        bz = bz + (at(wz, m + 9) - at(wz, m - 8))
        by = by + (at(wy, m + 9) - at(wy, m - 8))
        q = (m + 9) * 64
        s1[q : q + 64, :] = bz - 2.0 * t
        s2[q : q + 64, :] = by

    def at2(ref, i):
        if 0 <= i < 32:
            return ref[i * 64 : i * 64 + 64, :]
        return zero

    matt = myt[...]
    ge, go = zero, zero
    for k in range(48):
        ge = ge + (at2(s1, k) - at2(s1, k - 17))
        go = go + (at2(s2, k) - at2(s2, k - 17))
        both = jnp.concatenate(
            [jnp.concatenate([ge[r : r + 32], go[r : r + 32]], 0) for r in (0, 32)], 1
        )
        hi, lo = split(both)
        out = dot(matt, jnp.concatenate([hi, lo], 0))
        for p in range(2):
            z = slice(p * 128, p * 128 + 128)
            if 16 <= k < 32:
                n = (k - 16) * 2 + p
                low[n * 16 : n * 16 + 16, :] = out[0:16, z]
                own[n * 32 : n * 32 + 32, :] = out[16:48, z]
                high[n * 16 : n * 16 + 16, :] = out[48:64, z]
            else:
                n = (k if k < 16 else k - 16) * 2 + p
                hm[n * 32 : n * 32 + 16, :] = out[0:16, z]
                gm[n * 32 : n * 32 + 32, :] = out[16:48, z]
                hm[n * 32 + 16 : n * 32 + 32, :] = out[48:64, z]
    to_a = pl.ds(pl.multiple_of((1 - odd_core) * 1024, 1024), 1024)
    to_b = pl.ds(pl.multiple_of(odd_core * 1024, 1024), 1024)
    am[0:1024, :] = hm[to_a, :]
    am[1024:2048, :] = gm[to_a, :]
    hb[...] = hm[to_b, :]
    gb[...] = gm[to_b, :]


def base_kernel(d, c, xo, xe, xy, cy, edges, base, tly):
    left, right = masks("gx")
    for p in range(2):
        prev = None
        for j in range(17):
            f = SCALE * xo[j * 64 + p * 32 : j * 64 + p * 32 + 32, :]
            cl, cu = x_face_cells(edges, c, p, j, 64)
            lower, upper = face_sides(f, cl, cu, {0: left, 16: right}.get(j))
            if j:
                s = p * 512 + (j - 1) * 32
                base[s : s + 32, :] = cl + (lower + prev)
            prev = upper
    valid_y, valid_z = y_mask(), z_mask()
    for x in range(NX):
        for p in range(2):
            n = x * 2 + p
            t = n * 48
            f = (0.5 * SCALE) * xy[n * 40 : n * 40 + 40, :]
            lower, upper = face_sides(f, cy[t + 7 : t + 47, :], cy[t + 8 : t + 48, :], valid_y)
            tly[n * 40 : n * 40 + 40, :] = lower
            s = p * 512 + x * 32
            f = (0.5 * SCALE) * xe[n * 32 : n * 32 + 32, :]
            cl = c[s : s + 32, :]
            lower_z, upper_z = face_sides(f, cl, pltpu.roll(cl, NZ - 1, 1), valid_z)
            base[s : s + 32, :] = (
                base[s : s + 32, :] + upper[0:32, :] + (lower_z + pltpu.roll(upper_z, 1, 1))
            )
    for x in range(NX):
        for p in range(2):
            n = x * 2 + p
            s = p * 512 + x * 32
            base[s : s + 32, :] = base[s : s + 32, :] + tly[n * 40 + 1 : n * 40 + 33, :]


def margin_kernel(low, high, ha, hb, dn, up):
    for n in range(32):
        r, q = n * 16, n * 32
        dn[r : r + 16, :] = low[r : r + 16, :] + (ha[q : q + 16, :] + hb[q : q + 16, :])
        up[r : r + 16, :] = high[r : r + 16, :] + (ha[q + 16 : q + 32, :] + hb[q + 16 : q + 32, :])


def final_kernel(av, base, own, ga, gb, yl, yr, out):
    h = 0.5 * SCALE
    weights = [h * a for a in adhesion_rows(av)]
    for x in range(NX):
        pb = []
        for p in range(2):
            q = x * 32 + p * 16
            r = 2 * q
            got = jnp.concatenate([yl[q : q + 16, :], yr[q : q + 16, :]], 0)
            pb.append(own[r : r + 32, :] + (ga[1024 + r : 1056 + r, :] + gb[r : r + 32, :]) + got)
        for p in range(2):
            s = p * 512 + x * 32
            out[s : s + 32, :] = base[s : s + 32, :] + (
                weights[p] * pb[0] + weights[2 + p] * pb[1]
            )


def rows(n):
    return jax.ShapeDtypeStruct((n, 128), f32)


def scratch(n):
    return pltpu.VMEM((n, 128), f32)


def call(kernel, args, out_rows, scratch_rows=()):
    spec = pl.BlockSpec(memory_space=pltpu.VMEM)
    total = sum(a.shape[0] for a in args) + sum(out_rows) + sum(scratch_rows)
    single = len(out_rows) == 1
    shapes = [rows(n) for n in out_rows]
    return pl.pallas_call(
        kernel,
        out_shape=shapes[0] if single else shapes,
        in_specs=[spec] * len(args),
        out_specs=spec if single else [spec] * len(out_rows),
        scratch_shapes=[scratch(n) for n in scratch_rows],
        compiler_params=pltpu.CompilerParams(vmem_limit_bytes=total * 512 + (2 << 20)),
    )(*args)


def pack(d, c):
    spec = pl.BlockSpec(memory_space=pltpu.VMEM)
    return pl.pallas_call(
        pack_kernel,
        out_shape=[rows(YROWS), rows(YROWS), rows(1024), rows(1024)],
        in_specs=[pl.BlockSpec(memory_space=pltpu.HBM)] * 2,
        out_specs=[spec] * 4,
        scratch_shapes=[pltpu.SemaphoreType.DMA((8,))],
        compiler_params=pltpu.CompilerParams(vmem_limit_bytes=54_600_000),
    )(d, c)


def spread(adhesion):
    return pl.pallas_call(
        spread_kernel,
        out_shape=rows(32),
        in_specs=[pl.BlockSpec(memory_space=pltpu.SMEM)],
        out_specs=pl.BlockSpec(memory_space=pltpu.VMEM),
        compiler_params=pltpu.CompilerParams(vmem_limit_bytes=1 << 20),
    )(adhesion)


def shift(values, axis, by):
    n = lax.axis_size(axis)
    pairs = [(i, i + by) for i in range(n) if 0 <= i + by < n]
    return lax.ppermute(values, axis, pairs)


def swap(values, first):
    n = lax.axis_size("gx")
    pairs = []
    for i in range(first, n - 1, 2):
        pairs += [(i, i + 1), (i + 1, i)]
    return lax.ppermute(values, "gx", pairs)


def step(density, cotangent, adhesion):
    my = jnp.asarray(y_matrix(), bf16)
    myt = jnp.asarray(y_transposed(), bf16)
    ze, zo, zot = (jnp.asarray(m, bf16) for m in z_matrices())
    up, dn, d, c = pack(density.reshape(1024, 128), cotangent.reshape(1024, 128))
    yl = shift(up, "gy", 1)
    yr = shift(dn, "gy", -1)
    bb = swap(d, 1)
    ba = swap(d, 0)
    av = spread(adhesion)
    ma, mb, e0, e15 = call(
        corner_kernel, [av, d, c, yl, yr], [CROWS, CROWS, 128, 128]
    )
    kb = swap(mb, 1)
    ka = swap(ma, 0)
    r2l = shift(e15, "gx", 2)
    r2r = shift(e0, "gx", -2)
    seo, soo = call(y_own_kernel, [av, d, yl, yr, my], [1024, 1280], [512])
    own, low, high, am, gb, hb, xo, xe, xy, _, cy, edges = call(
        main_kernel,
        [av, d, c, yl, yr, ba, bb, ka, kb, r2l, r2r, seo, soo, my, ze, zo, zot, myt],
        [1024, 512, 512, 2048, 1024, 1024, 17 * 64, 1024, 1280, 1536, 1536, 256],
        [34 * 64, 32 * 80, 32 * 80, 34 * 64, 1280, 1024, 1024, 1024, 512, 2048, 2048],
    )
    hb2 = swap(hb, 1)
    gb2 = swap(gb, 1)
    am2 = swap(am, 0)
    dn2, up2 = call(margin_kernel, [low, high, am2, hb2], [512, 512])
    yl2 = shift(up2, "gy", 1)
    yr2 = shift(dn2, "gy", -1)
    base = call(base_kernel, [d, c, xo, xe, xy, cy, edges], [1024], [1280])
    out = call(final_kernel, [av, base, own, am2, gb2, yl2, yr2], [1024])
    return out.reshape(density.shape)


def solution(mesh):
    return jax.shard_map(
        step,
        mesh=mesh,
        in_specs=(P(None, "gx", "gy", None), P(None, "gx", "gy", None), P()),
        out_specs=P(None, "gx", "gy", None),
        check_vma=False,
    )
```

time: 82.2 us -> 79.1 us (0.962)
  the two profiles are of different devices: /device:TPU:111 before, /device:TPU:239 now
where the time goes in v2:
time: 79.1 us; the launch traced here: 78.5 us
  starting transfers between devices  38.5 us (49%)
  waiting for transfers between devices  29.9 us (38%)
  Pallas kernels  9.89 us (13%)
    ppermute x6, waiting for transfers between devices, shift(): return lax.ppermute(values, axis, pairs)  25 us
    ppermute x7, starting transfers between devices, swap(): return lax.ppermute(values, 'gx', pairs)  21.1 us
    ppermute x6, starting transfers between devices, shift(): return lax.ppermute(values, axis, pairs)  17.4 us
    pallas_call x6, Pallas kernels, call(): pl.pallas_call(kernel, out_shape=shapes[0] if single else shapes, in_spec...  7.97 us
    ppermute x7, waiting for transfers between devices, swap(): return lax.ppermute(values, 'gx', pairs)  4.94 us
  transfers between devices with their start and end apart: 13, of which 7 were waited for; matrix products, arithmetic and copies ran while one was open for 0% of the time, Pallas kernels for 3%

profile of v2, /device:TPU:239, one launch (start us, length us, event | category | flops | bytes accessed | tf_op | source)
XLA Modules:
  0.0 78.5 jit_solution(6430639414893437352)
XLA Ops:
  0.0 1.4 %shard_map.83 = (f32[576,128]{1,0:T(8,128)S(1)}, f32[576,128]{1,0:T(8,128)S(1)}, f32[1024,128]{1,0:T(8,128)S(1)}, f32[1024,128]{1,0:T(8,128)S(1)}) custom-call(f32[1024,128]{1,0:T(8,128)} %bitcast.3, f32[1024,128]{1,0:T(8,128)} %bitcast.4), custom_call_target="tpu_custom_call" | custom-call | tf_op jit(solution)/shard_map/pallas_call | solution.py:496
  1.4 0.0 copy-start.5
  1.4 3.1 %collective-permute-start = (f32[576,128]{1,0:T(8,128)S(1)}, f32[576,128]{1,0:T(8,128)S(1)}, u32[]{:S(2)}, u32[]{:S(2)}) collective-permute-start(f32[576,128]{1,0:T(8,128)S(1)} %get-tuple-element.30), channel_id=1, source_target_pairs={{0,1},{1,2},{2,3},{3,4},{4,5},{5,6},{6,7},{7,8},{8,9},{9,10},{10,1... | collective-permute-start | bytes 884744 | tf_op jit(solution)/shard_map/ppermute | solution.py:519
  4.5 2.2 %collective-permute-start.1 = (f32[576,128]{1,0:T(8,128)S(1)}, f32[576,128]{1,0:T(8,128)S(1)}, u32[]{:S(2)}, u32[]{:S(2)}) collective-permute-start(f32[576,128]{1,0:T(8,128)S(1)} %get-tuple-element.31), channel_id=1, source_target_pairs={{1,0},{2,1},{3,2},{4,3},{5,4},{6,5},{7,6},{8,7},{9,8},{10,9},{11,1... | collective-permute-start | bytes 884744 | tf_op jit(solution)/shard_map/ppermute | solution.py:519
  6.7 0.0 copy-done.5
  6.7 0.6 shard_map.82.av
  7.3 3.9 %collective-permute-done.yl = f32[576,128]{1,0:T(8,128)S(1)} collective-permute-done((f32[576,128]{1,0:T(8,128)S(1)}, f32[576,128]{1,0:T(8,128)S(1)}, u32[]{:S(2)}, u32[]{:S(2)}) %collective-permute-start) | collective-permute-done | bytes 294944 | tf_op jit(solution)/shard_map/ppermute | solution.py:519
  11.2 5.0 %collective-permute-done.1.yr = f32[576,128]{1,0:T(8,128)S(1)} collective-permute-done((f32[576,128]{1,0:T(8,128)S(1)}, f32[576,128]{1,0:T(8,128)S(1)}, u32[]{:S(2)}, u32[]{:S(2)}) %collective-permute-start.1) | collective-permute-done | bytes 294944 | tf_op jit(solution)/shard_map/ppermute | solution.py:519
  16.1 0.0 copy-start
  16.1 0.1 shard_map.84
  16.2 3.7 %collective-permute-start.4 = (f32[1152,128]{1,0:T(8,128)S(1)}, f32[1152,128]{1,0:T(8,128)S(1)}, u32[]{:S(2)}, u32[]{:S(2)}) collective-permute-start(f32[1152,128]{1,0:T(8,128)S(1)} %get-tuple-element.32), channel_id=1, source_target_pairs={{0,16},{16,0},{32,48},{48,32},{64,80},{80,64},{96,112},{112,96},{1... | collective-permute-start | bytes 1769480 | tf_op jit(solution)/shard_map/ppermute | solution.py:527
  20.0 4.7 %collective-permute-start.5 = (f32[1152,128]{1,0:T(8,128)S(1)}, f32[1152,128]{1,0:T(8,128)S(1)}, u32[]{:S(2)}, u32[]{:S(2)}) collective-permute-start(f32[1152,128]{1,0:T(8,128)S(1)} %get-tuple-element.33), channel_id=1, source_target_pairs={{16,32},{32,16},{48,64},{64,48},{80,96},{96,80},{112,128},{128,112... | collective-permute-start | bytes 1769480 | tf_op jit(solution)/shard_map/ppermute | solution.py:527
  24.6 2.1 %collective-permute-start.3 = (f32[1024,128]{1,0:T(8,128)S(1)}, f32[1024,128]{1,0:T(8,128)S(1)}, u32[]{:S(2)}, u32[]{:S(2)}) collective-permute-start(f32[1024,128]{1,0:T(8,128)S(1)} %get-tuple-element.28.d), channel_id=1, source_target_pairs={{16,32},{32,16},{48,64},{64,48},{80,96},{96,80},{112,128},{128,112... | collective-permute-start | bytes 1572872 | tf_op jit(solution)/shard_map/ppermute | solution.py:527
  26.7 1.9 %collective-permute-start.2 = (f32[1024,128]{1,0:T(8,128)S(1)}, f32[1024,128]{1,0:T(8,128)S(1)}, u32[]{:S(2)}, u32[]{:S(2)}) collective-permute-start(f32[1024,128]{1,0:T(8,128)S(1)} %get-tuple-element.28.d), channel_id=1, source_target_pairs={{0,16},{16,0},{32,48},{48,32},{64,80},{80,64},{96,112},{112,96},{1... | collective-permute-start | bytes 1572872 | tf_op jit(solution)/shard_map/ppermute | solution.py:527
  28.7 4.8 %collective-permute-start.6 = (f32[128,128]{1,0:T(8,128)S(1)}, f32[128,128]{1,0:T(8,128)S(1)}, u32[]{:S(2)}, u32[]{:S(2)}) collective-permute-start(f32[128,128]{1,0:T(8,128)S(1)} %get-tuple-element.34), channel_id=1, source_target_pairs={{0,32},{16,48},{32,64},{48,80},{64,96},{80,112},{96,128},{112,144}... | collective-permute-start | bytes 196616 | tf_op jit(solution)/shard_map/ppermute | solution.py:519
  33.4 5.0 %collective-permute-done.6.r2l = f32[128,128]{1,0:T(8,128)S(1)} collective-permute-done((f32[128,128]{1,0:T(8,128)S(1)}, f32[128,128]{1,0:T(8,128)S(1)}, u32[]{:S(2)}, u32[]{:S(2)}) %collective-permute-start.6) | collective-permute-done | bytes 65568 | tf_op jit(solution)/shard_map/ppermute | solution.py:519
  38.4 0.0 copy-start.1
  38.4 0.0 copy-start.2
  38.4 0.0 copy-start.3
  38.4 0.0 copy-start.4
  38.5 2.0 %collective-permute-start.7 = (f32[128,128]{1,0:T(8,128)S(1)}, f32[128,128]{1,0:T(8,128)S(1)}, u32[]{:S(2)}, u32[]{:S(2)}) collective-permute-start(f32[128,128]{1,0:T(8,128)S(1)} %get-tuple-element.35), channel_id=1, source_target_pairs={{32,0},{48,16},{64,32},{80,48},{96,64},{112,80},{128,96},{144,112}... | collective-permute-start | bytes 196616 | tf_op jit(solution)/shard_map/ppermute | solution.py:519
  40.5 0.0 copy-done
  40.5 0.5 shard_map.85
  41.0 4.3 %collective-permute-done.7.r2r = f32[128,128]{1,0:T(8,128)S(1)} collective-permute-done((f32[128,128]{1,0:T(8,128)S(1)}, f32[128,128]{1,0:T(8,128)S(1)}, u32[]{:S(2)}, u32[]{:S(2)}) %collective-permute-start.7) | collective-permute-done | bytes 65568 | tf_op jit(solution)/shard_map/ppermute | solution.py:519
  45.3 0.0 collective-permute-done.3.bb
  45.3 0.0 collective-permute-done.2.ba
  45.3 0.0 collective-permute-done.4.ka
  45.3 0.0 collective-permute-done.5.kb
  45.3 0.0 copy-done.1
  45.3 0.0 copy-done.2
  45.3 0.0 copy-done.3
  45.3 0.0 copy-done.4
  45.3 4.8 %shard_map.86 = (f32[1024,128]{1,0:T(8,128)S(1)}, f32[512,128]{1,0:T(8,128)S(1)}, f32[512,128]{1,0:T(8,128)S(1)}, f32[2048,128]{1,0:T(8,128)S(1)}, f32[1024,128]...) custom-call(f32[32,128]{1,0:T(8,128)S(1)} %shard_map.82.av, ...), custom_call_target="tpu_custom_call" | custom-call | tf_op jit(solution)/shard_map/pallas_call | solution.py:484
  50.1 1.9 %collective-permute-start.8 = (f32[2048,128]{1,0:T(8,128)S(1)}, f32[2048,128]{1,0:T(8,128)S(1)}, u32[]{:S(2)}, u32[]{:S(2)}) collective-permute-start(f32[2048,128]{1,0:T(8,128)S(1)} %get-tuple-element.44), channel_id=1, source_target_pairs={{0,16},{16,0},{32,48},{48,32},{64,80},{80,64},{96,112},{112,96},{1... | collective-permute-start | bytes 3145736 | tf_op jit(solution)/shard_map/ppermute | solution.py:527
  52.1 3.7 %collective-permute-start.10 = (f32[1024,128]{1,0:T(8,128)S(1)}, f32[1024,128]{1,0:T(8,128)S(1)}, u32[]{:S(2)}, u32[]{:S(2)}) collective-permute-start(f32[1024,128]{1,0:T(8,128)S(1)} %get-tuple-element.48), channel_id=1, source_target_pairs={{16,32},{32,16},{48,64},{64,48},{80,96},{96,80},{112,128},{128,112... | collective-permute-start | bytes 1572872 | tf_op jit(solution)/shard_map/ppermute | solution.py:527
  55.8 3.0 %collective-permute-start.9 = (f32[1024,128]{1,0:T(8,128)S(1)}, f32[1024,128]{1,0:T(8,128)S(1)}, u32[]{:S(2)}, u32[]{:S(2)}) collective-permute-start(f32[1024,128]{1,0:T(8,128)S(1)} %get-tuple-element.45), channel_id=1, source_target_pairs={{16,32},{32,16},{48,64},{64,48},{80,96},{96,80},{112,128},{128,112... | collective-permute-start | bytes 1572872 | tf_op jit(solution)/shard_map/ppermute | solution.py:527
  58.9 4.9 %collective-permute-done.10.hb = f32[1024,128]{1,0:T(8,128)S(1)} collective-permute-done((f32[1024,128]{1,0:T(8,128)S(1)}, f32[1024,128]{1,0:T(8,128)S(1)}, u32[]{:S(2)}, u32[]{:S(2)}) %collective-permute-start.10) | collective-permute-done | bytes 524320 | tf_op jit(solution)/shard_map/ppermute | solution.py:527
  63.8 0.0 collective-permute-done.8.ha.ga
  63.8 0.1 shard_map.88
  63.9 1.9 %collective-permute-start.11 = (f32[512,128]{1,0:T(8,128)S(1)}, f32[512,128]{1,0:T(8,128)S(1)}, u32[]{:S(2)}, u32[]{:S(2)}) collective-permute-start(f32[512,128]{1,0:T(8,128)S(1)} %get-tuple-element.49), channel_id=1, source_target_pairs={{0,1},{1,2},{2,3},{3,4},{4,5},{5,6},{6,7},{7,8},{8,9},{9,10},{10,1... | collective-permute-start | bytes 786440 | tf_op jit(solution)/shard_map/ppermute | solution.py:519
  65.8 3.4 %collective-permute-start.12 = (f32[512,128]{1,0:T(8,128)S(1)}, f32[512,128]{1,0:T(8,128)S(1)}, u32[]{:S(2)}, u32[]{:S(2)}) collective-permute-start(f32[512,128]{1,0:T(8,128)S(1)} %get-tuple-element.50), channel_id=1, source_target_pairs={{1,0},{2,1},{3,2},{4,3},{5,4},{6,5},{7,6},{8,7},{9,8},{10,9},{11,1... | collective-permute-start | bytes 786440 | tf_op jit(solution)/shard_map/ppermute | solution.py:519
  69.2 1.6 %shard_map.87.base = f32[1024,128]{1,0:T(8,128)S(1)} custom-call(f32[1024,128]{1,0:T(8,128)S(1)} %get-tuple-element.28.d, f32[1024,128]{1,0:T(8,128)S(1)} %get-tuple-element.29.c, f32[1088,128]{1,0:T(8,128)S(1)} %get-tuple-element.38.xo, f32[1024,128]{1,0:T(8,128)S(1)} %get-tuple-element.39.xe, f32[1280,128]{1,0:T(8,128)S(1)} %get-tuple-element.40.xy, ...), custom_call_target="tpu_custom_call" | custom-call | tf_op jit(solution)/shard_map/pallas_call | solution.py:484
  70.8 0.0 collective-permute-done.9.gb
  70.8 3.0 %collective-permute-done.11.yl = f32[512,128]{1,0:T(8,128)S(1)} collective-permute-done((f32[512,128]{1,0:T(8,128)S(1)}, f32[512,128]{1,0:T(8,128)S(1)}, u32[]{:S(2)}, u32[]{:S(2)}) %collective-permute-start.11) | collective-permute-done | bytes 262176 | tf_op jit(solution)/shard_map/ppermute | solution.py:519
  73.8 3.8 %collective-permute-done.12.yr = f32[512,128]{1,0:T(8,128)S(1)} collective-permute-done((f32[512,128]{1,0:T(8,128)S(1)}, f32[512,128]{1,0:T(8,128)S(1)}, u32[]{:S(2)}, u32[]{:S(2)}) %collective-permute-start.12) | collective-permute-done | bytes 262176 | tf_op jit(solution)/shard_map/ppermute | solution.py:519
  77.6 0.9 %shard_map.89 = f32[1024,128]{1,0:T(8,128)} custom-call(f32[32,128]{1,0:T(8,128)S(1)} %shard_map.82.av, f32[1024,128]{1,0:T(8,128)S(1)} %shard_map.87.base, f32[1024,128]{1,0:T(8,128)S(1)} %get-tuple-element.43.own, f32[2048,128]{1,0:T(8,128)S(1)} %collective-permute-done.8.ha.ga, f32[1024,128]{1,0:T(8,128)S(1)} %collective-permute-done.9.gb, ...), custom_call_target="tpu_custom_call" | custom-call | tf_op jit(solution)/shard_map/pallas_call | solution.py:484
Async XLA Ops:
  1.4 5.3 %copy-start.5 = (f32[2,2]{1,0:T(2,128)S(1)}, f32[2,2]{1,0:T(2,128)}, u32[]{:S(2)}) copy-start(f32[2,2]{1,0:T(2,128)} %adh.1) | copy-start | bytes 52
  1.4 9.8 %collective-permute-start = (f32[576,128]{1,0:T(8,128)S(1)}, f32[576,128]{1,0:T(8,128)S(1)}, u32[]{:S(2)}, u32[]{:S(2)}) collective-permute-start(f32[576,128]{1,0:T(8,128)S(1)} %get-tuple-element.30), channel_id=1, source_target_pairs={{0,1},{1,2},{2,3},{3,4},{4,5},{5,6},{6,7},{7,8},{8,9},{9,10},{10,1... | collective-permute-start | bytes 884744 | tf_op jit(solution)/shard_map/ppermute | solution.py:519
  4.5 11.6 %collective-permute-start.1 = (f32[576,128]{1,0:T(8,128)S(1)}, f32[576,128]{1,0:T(8,128)S(1)}, u32[]{:S(2)}, u32[]{:S(2)}) collective-permute-start(f32[576,128]{1,0:T(8,128)S(1)} %get-tuple-element.31), channel_id=1, source_target_pairs={{1,0},{2,1},{3,2},{4,3},{5,4},{6,5},{7,6},{8,7},{9,8},{10,9},{11,1... | collective-permute-start | bytes 884744 | tf_op jit(solution)/shard_map/ppermute | solution.py:519
  16.1 24.4 %copy-start = (bf16[80,160]{1,0:T(8,128)(2,1)S(1)}, bf16[80,160]{1,0:T(8,128)(2,1)}, u32[]{:S(2)}) copy-start(bf16[80,160]{1,0:T(8,128)(2,1)} %constant.10.clone.my) | copy-start | bytes 76804
  16.2 29.0 %collective-permute-start.4 = (f32[1152,128]{1,0:T(8,128)S(1)}, f32[1152,128]{1,0:T(8,128)S(1)}, u32[]{:S(2)}, u32[]{:S(2)}) collective-permute-start(f32[1152,128]{1,0:T(8,128)S(1)} %get-tuple-element.32), channel_id=1, source_target_pairs={{0,16},{16,0},{32,48},{48,32},{64,80},{80,64},{96,112},{112,96},{1... | collective-permute-start | bytes 1769480 | tf_op jit(solution)/shard_map/ppermute | solution.py:527
  20.0 25.3 %collective-permute-start.5 = (f32[1152,128]{1,0:T(8,128)S(1)}, f32[1152,128]{1,0:T(8,128)S(1)}, u32[]{:S(2)}, u32[]{:S(2)}) collective-permute-start(f32[1152,128]{1,0:T(8,128)S(1)} %get-tuple-element.33), channel_id=1, source_target_pairs={{16,32},{32,16},{48,64},{64,48},{80,96},{96,80},{112,128},{128,112... | collective-permute-start | bytes 1769480 | tf_op jit(solution)/shard_map/ppermute | solution.py:527
  24.6 20.6 %collective-permute-start.3 = (f32[1024,128]{1,0:T(8,128)S(1)}, f32[1024,128]{1,0:T(8,128)S(1)}, u32[]{:S(2)}, u32[]{:S(2)}) collective-permute-start(f32[1024,128]{1,0:T(8,128)S(1)} %get-tuple-element.28.d), channel_id=1, source_target_pairs={{16,32},{32,16},{48,64},{64,48},{80,96},{96,80},{112,128},{128,112... | collective-permute-start | bytes 1572872 | tf_op jit(solution)/shard_map/ppermute | solution.py:527
  26.7 18.5 %collective-permute-start.2 = (f32[1024,128]{1,0:T(8,128)S(1)}, f32[1024,128]{1,0:T(8,128)S(1)}, u32[]{:S(2)}, u32[]{:S(2)}) collective-permute-start(f32[1024,128]{1,0:T(8,128)S(1)} %get-tuple-element.28.d), channel_id=1, source_target_pairs={{0,16},{16,0},{32,48},{48,32},{64,80},{80,64},{96,112},{112,96},{1... | collective-permute-start | bytes 1572872 | tf_op jit(solution)/shard_map/ppermute | solution.py:527
  28.7 9.8 %collective-permute-start.6 = (f32[128,128]{1,0:T(8,128)S(1)}, f32[128,128]{1,0:T(8,128)S(1)}, u32[]{:S(2)}, u32[]{:S(2)}) collective-permute-start(f32[128,128]{1,0:T(8,128)S(1)} %get-tuple-element.34), channel_id=1, source_target_pairs={{0,32},{16,48},{32,64},{48,80},{64,96},{80,112},{96,128},{112,144}... | collective-permute-start | bytes 196616 | tf_op jit(solution)/shard_map/ppermute | solution.py:519
  38.4 6.8 %copy-start.1 = (bf16[256,128]{1,0:T(8,128)(2,1)S(1)}, bf16[256,128]{1,0:T(8,128)(2,1)}, u32[]{:S(2)}) copy-start(bf16[256,128]{1,0:T(8,128)(2,1)} %constant.14.clone.zot) | copy-start | bytes 196612
  38.4 6.8 %copy-start.2 = (bf16[256,128]{1,0:T(8,128)(2,1)S(1)}, bf16[256,128]{1,0:T(8,128)(2,1)}, u32[]{:S(2)}) copy-start(bf16[256,128]{1,0:T(8,128)(2,1)} %constant.13.clone.zo) | copy-start | bytes 196612
  38.4 6.9 %copy-start.3 = (bf16[256,128]{1,0:T(8,128)(2,1)S(1)}, bf16[256,128]{1,0:T(8,128)(2,1)}, u32[]{:S(2)}) copy-start(bf16[256,128]{1,0:T(8,128)(2,1)} %constant.12.clone.ze) | copy-start | bytes 196612
  38.4 6.9 %copy-start.4 = (bf16[64,128]{1,0:T(8,128)(2,1)S(1)}, bf16[64,128]{1,0:T(8,128)(2,1)}, u32[]{:S(2)}) copy-start(bf16[64,128]{1,0:T(8,128)(2,1)} %constant.11.clone.myt) | copy-start | bytes 49156
  38.5 6.8 %collective-permute-start.7 = (f32[128,128]{1,0:T(8,128)S(1)}, f32[128,128]{1,0:T(8,128)S(1)}, u32[]{:S(2)}, u32[]{:S(2)}) collective-permute-start(f32[128,128]{1,0:T(8,128)S(1)} %get-tuple-element.35), channel_id=1, source_target_pairs={{32,0},{48,16},{64,32},{80,48},{96,64},{112,80},{128,96},{144,112}... | collective-permute-start | bytes 196616 | tf_op jit(solution)/shard_map/ppermute | solution.py:519
  50.1 13.6 %collective-permute-start.8 = (f32[2048,128]{1,0:T(8,128)S(1)}, f32[2048,128]{1,0:T(8,128)S(1)}, u32[]{:S(2)}, u32[]{:S(2)}) collective-permute-start(f32[2048,128]{1,0:T(8,128)S(1)} %get-tuple-element.44), channel_id=1, source_target_pairs={{0,16},{16,0},{32,48},{48,32},{64,80},{80,64},{96,112},{112,96},{1... | collective-permute-start | bytes 3145736 | tf_op jit(solution)/shard_map/ppermute | solution.py:527
  52.1 11.7 %collective-permute-start.10 = (f32[1024,128]{1,0:T(8,128)S(1)}, f32[1024,128]{1,0:T(8,128)S(1)}, u32[]{:S(2)}, u32[]{:S(2)}) collective-permute-start(f32[1024,128]{1,0:T(8,128)S(1)} %get-tuple-element.48), channel_id=1, source_target_pairs={{16,32},{32,16},{48,64},{64,48},{80,96},{96,80},{112,128},{128,112... | collective-permute-start | bytes 1572872 | tf_op jit(solution)/shard_map/ppermute | solution.py:527
  55.8 15.0 %collective-permute-start.9 = (f32[1024,128]{1,0:T(8,128)S(1)}, f32[1024,128]{1,0:T(8,128)S(1)}, u32[]{:S(2)}, u32[]{:S(2)}) collective-permute-start(f32[1024,128]{1,0:T(8,128)S(1)} %get-tuple-element.45), channel_id=1, source_target_pairs={{16,32},{32,16},{48,64},{64,48},{80,96},{96,80},{112,128},{128,112... | collective-permute-start | bytes 1572872 | tf_op jit(solution)/shard_map/ppermute | solution.py:527
  63.9 10.0 %collective-permute-start.11 = (f32[512,128]{1,0:T(8,128)S(1)}, f32[512,128]{1,0:T(8,128)S(1)}, u32[]{:S(2)}, u32[]{:S(2)}) collective-permute-start(f32[512,128]{1,0:T(8,128)S(1)} %get-tuple-element.49), channel_id=1, source_target_pairs={{0,1},{1,2},{2,3},{3,4},{4,5},{5,6},{6,7},{7,8},{8,9},{9,10},{10,1... | collective-permute-start | bytes 786440 | tf_op jit(solution)/shard_map/ppermute | solution.py:519
  65.8 11.8 %collective-permute-start.12 = (f32[512,128]{1,0:T(8,128)S(1)}, f32[512,128]{1,0:T(8,128)S(1)}, u32[]{:S(2)}, u32[]{:S(2)}) collective-permute-start(f32[512,128]{1,0:T(8,128)S(1)} %get-tuple-element.50), channel_id=1, source_target_pairs={{1,0},{2,1},{3,2},{4,3},{5,4},{6,5},{7,6},{8,7},{9,8},{10,9},{11,1... | collective-permute-start | bytes 786440 | tf_op jit(solution)/shard_map/ppermute | solution.py:519

commit v3 on v2

--- a/solution.py
+++ b/solution.py
@@ -216,8 +216,8 @@
 
 def main_kernel(
     av, d, c, yl, yr, ba, bb, ka, kb, r2l, r2r, seo, soo, my, ze, zo, zot, myt,
-    own, low, high, am, gb, hb, xo, xe, xy, dy, cy, edges,
-    se, so, s1, s2, vby, wx, wy, wz, ext, gm, hm,
+    own, low, high, am, gb, hb, xo, xe, xy, cy, edges,
+    dy, se, so, s1, s2, vby, wx, wy, wz, ext, gm, hm,
 ):
     odd_core = lax.rem(lax.axis_index("gx"), 2)
     left, right = masks("gx")
@@ -545,11 +545,11 @@
     r2l = shift(e15, "gx", 2)
     r2r = shift(e0, "gx", -2)
     seo, soo = call(y_own_kernel, [av, d, yl, yr, my], [1024, 1280], [512])
-    own, low, high, am, gb, hb, xo, xe, xy, _, cy, edges = call(
+    own, low, high, am, gb, hb, xo, xe, xy, cy, edges = call(
         main_kernel,
         [av, d, c, yl, yr, ba, bb, ka, kb, r2l, r2r, seo, soo, my, ze, zo, zot, myt],
-        [1024, 512, 512, 2048, 1024, 1024, 17 * 64, 1024, 1280, 1536, 1536, 256],
-        [34 * 64, 32 * 80, 32 * 80, 34 * 64, 1280, 1024, 1024, 1024, 512, 2048, 2048],
+        [1024, 512, 512, 2048, 1024, 1024, 17 * 64, 1024, 1280, 1536, 256],
+        [1536, 34 * 64, 32 * 80, 32 * 80, 34 * 64, 1280, 1024, 1024, 1024, 512, 2048, 2048],
     )
     hb2 = swap(hb, 1)
     gb2 = swap(gb, 1)

time: 79.1 us -> 78.9 us (level)
  the two profiles are of different devices: /device:TPU:239 before, /device:TPU:111 now
where the time goes in v3:
time: 78.9 us; the launch traced here: 78.4 us
  starting transfers between devices  38.5 us (49%)
  waiting for transfers between devices  29.9 us (38%)
  Pallas kernels  9.79 us (12%)
    ppermute x6, waiting for transfers between devices, shift(): return lax.ppermute(values, axis, pairs)  25 us
    ppermute x7, starting transfers between devices, swap(): return lax.ppermute(values, 'gx', pairs)  21.1 us
    ppermute x6, starting transfers between devices, shift(): return lax.ppermute(values, axis, pairs)  17.4 us
    pallas_call x6, Pallas kernels, call(): pl.pallas_call(kernel, out_shape=shapes[0] if single else shapes, in_spec...  7.87 us
    ppermute x7, waiting for transfers between devices, swap(): return lax.ppermute(values, 'gx', pairs)  4.94 us
  transfers between devices with their start and end apart: 13, of which 7 were waited for; matrix products, arithmetic and copies ran while one was open for 0% of the time, Pallas kernels for 3%

profile of v3, /device:TPU:111, one launch (start us, length us, event | category | flops | bytes accessed | tf_op | source)
XLA Modules:
  0.0 78.4 jit_solution(3716211036969901883)
XLA Ops:
  0.0 1.4 %shard_map.83 = (f32[576,128]{1,0:T(8,128)S(1)}, f32[576,128]{1,0:T(8,128)S(1)}, f32[1024,128]{1,0:T(8,128)S(1)}, f32[1024,128]{1,0:T(8,128)S(1)}) custom-call(f32[1024,128]{1,0:T(8,128)} %bitcast.3, f32[1024,128]{1,0:T(8,128)} %bitcast.4), custom_call_target="tpu_custom_call" | custom-call | tf_op jit(solution)/shard_map/pallas_call | solution.py:496
  1.4 0.0 copy-start.5
  1.4 3.1 %collective-permute-start = (f32[576,128]{1,0:T(8,128)S(1)}, f32[576,128]{1,0:T(8,128)S(1)}, u32[]{:S(2)}, u32[]{:S(2)}) collective-permute-start(f32[576,128]{1,0:T(8,128)S(1)} %get-tuple-element.30), channel_id=1, source_target_pairs={{0,1},{1,2},{2,3},{3,4},{4,5},{5,6},{6,7},{7,8},{8,9},{9,10},{10,1... | collective-permute-start | bytes 884744 | tf_op jit(solution)/shard_map/ppermute | solution.py:519
  4.5 2.2 %collective-permute-start.1 = (f32[576,128]{1,0:T(8,128)S(1)}, f32[576,128]{1,0:T(8,128)S(1)}, u32[]{:S(2)}, u32[]{:S(2)}) collective-permute-start(f32[576,128]{1,0:T(8,128)S(1)} %get-tuple-element.31), channel_id=1, source_target_pairs={{1,0},{2,1},{3,2},{4,3},{5,4},{6,5},{7,6},{8,7},{9,8},{10,9},{11,1... | collective-permute-start | bytes 884744 | tf_op jit(solution)/shard_map/ppermute | solution.py:519
  6.7 0.0 copy-done.5
  6.7 0.6 shard_map.82.av
  7.3 3.9 %collective-permute-done.yl = f32[576,128]{1,0:T(8,128)S(1)} collective-permute-done((f32[576,128]{1,0:T(8,128)S(1)}, f32[576,128]{1,0:T(8,128)S(1)}, u32[]{:S(2)}, u32[]{:S(2)}) %collective-permute-start) | collective-permute-done | bytes 294944 | tf_op jit(solution)/shard_map/ppermute | solution.py:519
  11.2 5.0 %collective-permute-done.1.yr = f32[576,128]{1,0:T(8,128)S(1)} collective-permute-done((f32[576,128]{1,0:T(8,128)S(1)}, f32[576,128]{1,0:T(8,128)S(1)}, u32[]{:S(2)}, u32[]{:S(2)}) %collective-permute-start.1) | collective-permute-done | bytes 294944 | tf_op jit(solution)/shard_map/ppermute | solution.py:519
  16.1 0.0 copy-start
  16.1 0.1 shard_map.84
  16.2 3.7 %collective-permute-start.4 = (f32[1152,128]{1,0:T(8,128)S(1)}, f32[1152,128]{1,0:T(8,128)S(1)}, u32[]{:S(2)}, u32[]{:S(2)}) collective-permute-start(f32[1152,128]{1,0:T(8,128)S(1)} %get-tuple-element.32), channel_id=1, source_target_pairs={{0,16},{16,0},{32,48},{48,32},{64,80},{80,64},{96,112},{112,96},{1... | collective-permute-start | bytes 1769480 | tf_op jit(solution)/shard_map/ppermute | solution.py:527
  20.0 4.7 %collective-permute-start.5 = (f32[1152,128]{1,0:T(8,128)S(1)}, f32[1152,128]{1,0:T(8,128)S(1)}, u32[]{:S(2)}, u32[]{:S(2)}) collective-permute-start(f32[1152,128]{1,0:T(8,128)S(1)} %get-tuple-element.33), channel_id=1, source_target_pairs={{16,32},{32,16},{48,64},{64,48},{80,96},{96,80},{112,128},{128,112... | collective-permute-start | bytes 1769480 | tf_op jit(solution)/shard_map/ppermute | solution.py:527
  24.6 2.1 %collective-permute-start.3 = (f32[1024,128]{1,0:T(8,128)S(1)}, f32[1024,128]{1,0:T(8,128)S(1)}, u32[]{:S(2)}, u32[]{:S(2)}) collective-permute-start(f32[1024,128]{1,0:T(8,128)S(1)} %get-tuple-element.28.d), channel_id=1, source_target_pairs={{16,32},{32,16},{48,64},{64,48},{80,96},{96,80},{112,128},{128,112... | collective-permute-start | bytes 1572872 | tf_op jit(solution)/shard_map/ppermute | solution.py:527
  26.7 1.9 %collective-permute-start.2 = (f32[1024,128]{1,0:T(8,128)S(1)}, f32[1024,128]{1,0:T(8,128)S(1)}, u32[]{:S(2)}, u32[]{:S(2)}) collective-permute-start(f32[1024,128]{1,0:T(8,128)S(1)} %get-tuple-element.28.d), channel_id=1, source_target_pairs={{0,16},{16,0},{32,48},{48,32},{64,80},{80,64},{96,112},{112,96},{1... | collective-permute-start | bytes 1572872 | tf_op jit(solution)/shard_map/ppermute | solution.py:527
  28.7 4.8 %collective-permute-start.6 = (f32[128,128]{1,0:T(8,128)S(1)}, f32[128,128]{1,0:T(8,128)S(1)}, u32[]{:S(2)}, u32[]{:S(2)}) collective-permute-start(f32[128,128]{1,0:T(8,128)S(1)} %get-tuple-element.34), channel_id=1, source_target_pairs={{0,32},{16,48},{32,64},{48,80},{64,96},{80,112},{96,128},{112,144}... | collective-permute-start | bytes 196616 | tf_op jit(solution)/shard_map/ppermute | solution.py:519
  33.4 5.0 %collective-permute-done.6.r2l = f32[128,128]{1,0:T(8,128)S(1)} collective-permute-done((f32[128,128]{1,0:T(8,128)S(1)}, f32[128,128]{1,0:T(8,128)S(1)}, u32[]{:S(2)}, u32[]{:S(2)}) %collective-permute-start.6) | collective-permute-done | bytes 65568 | tf_op jit(solution)/shard_map/ppermute | solution.py:519
  38.4 0.0 copy-start.1
  38.4 0.0 copy-start.2
  38.4 0.0 copy-start.3
  38.4 0.0 copy-start.4
  38.5 2.0 %collective-permute-start.7 = (f32[128,128]{1,0:T(8,128)S(1)}, f32[128,128]{1,0:T(8,128)S(1)}, u32[]{:S(2)}, u32[]{:S(2)}) collective-permute-start(f32[128,128]{1,0:T(8,128)S(1)} %get-tuple-element.35), channel_id=1, source_target_pairs={{32,0},{48,16},{64,32},{80,48},{96,64},{112,80},{128,96},{144,112}... | collective-permute-start | bytes 196616 | tf_op jit(solution)/shard_map/ppermute | solution.py:519
  40.5 0.0 copy-done
  40.5 0.5 shard_map.85
  41.0 4.3 %collective-permute-done.7.r2r = f32[128,128]{1,0:T(8,128)S(1)} collective-permute-done((f32[128,128]{1,0:T(8,128)S(1)}, f32[128,128]{1,0:T(8,128)S(1)}, u32[]{:S(2)}, u32[]{:S(2)}) %collective-permute-start.7) | collective-permute-done | bytes 65568 | tf_op jit(solution)/shard_map/ppermute | solution.py:519
  45.3 0.0 collective-permute-done.3.bb
  45.3 0.0 collective-permute-done.2.ba
  45.3 0.0 collective-permute-done.4.ka
  45.3 0.0 collective-permute-done.5.kb
  45.3 0.0 copy-done.1
  45.3 0.0 copy-done.2
  45.3 0.0 copy-done.3
  45.3 0.0 copy-done.4
  45.3 4.7 %shard_map.86 = (f32[1024,128]{1,0:T(8,128)S(1)}, f32[512,128]{1,0:T(8,128)S(1)}, f32[512,128]{1,0:T(8,128)S(1)}, f32[2048,128]{1,0:T(8,128)S(1)}, f32[1024,128]...) custom-call(f32[32,128]{1,0:T(8,128)S(1)} %shard_map.82.av, ...), custom_call_target="tpu_custom_call" | custom-call | tf_op jit(solution)/shard_map/pallas_call | solution.py:484
  50.0 1.9 %collective-permute-start.8 = (f32[2048,128]{1,0:T(8,128)S(1)}, f32[2048,128]{1,0:T(8,128)S(1)}, u32[]{:S(2)}, u32[]{:S(2)}) collective-permute-start(f32[2048,128]{1,0:T(8,128)S(1)} %get-tuple-element.44), channel_id=1, source_target_pairs={{0,16},{16,0},{32,48},{48,32},{64,80},{80,64},{96,112},{112,96},{1... | collective-permute-start | bytes 3145736 | tf_op jit(solution)/shard_map/ppermute | solution.py:527
  52.0 3.7 %collective-permute-start.10 = (f32[1024,128]{1,0:T(8,128)S(1)}, f32[1024,128]{1,0:T(8,128)S(1)}, u32[]{:S(2)}, u32[]{:S(2)}) collective-permute-start(f32[1024,128]{1,0:T(8,128)S(1)} %get-tuple-element.48), channel_id=1, source_target_pairs={{16,32},{32,16},{48,64},{64,48},{80,96},{96,80},{112,128},{128,112... | collective-permute-start | bytes 1572872 | tf_op jit(solution)/shard_map/ppermute | solution.py:527
  55.7 3.0 %collective-permute-start.9 = (f32[1024,128]{1,0:T(8,128)S(1)}, f32[1024,128]{1,0:T(8,128)S(1)}, u32[]{:S(2)}, u32[]{:S(2)}) collective-permute-start(f32[1024,128]{1,0:T(8,128)S(1)} %get-tuple-element.45), channel_id=1, source_target_pairs={{16,32},{32,16},{48,64},{64,48},{80,96},{96,80},{112,128},{128,112... | collective-permute-start | bytes 1572872 | tf_op jit(solution)/shard_map/ppermute | solution.py:527
  58.7 4.9 %collective-permute-done.10.hb = f32[1024,128]{1,0:T(8,128)S(1)} collective-permute-done((f32[1024,128]{1,0:T(8,128)S(1)}, f32[1024,128]{1,0:T(8,128)S(1)}, u32[]{:S(2)}, u32[]{:S(2)}) %collective-permute-start.10) | collective-permute-done | bytes 524320 | tf_op jit(solution)/shard_map/ppermute | solution.py:527
  63.7 0.0 collective-permute-done.8.ha.ga
  63.7 0.1 shard_map.88
  63.8 1.9 %collective-permute-start.11 = (f32[512,128]{1,0:T(8,128)S(1)}, f32[512,128]{1,0:T(8,128)S(1)}, u32[]{:S(2)}, u32[]{:S(2)}) collective-permute-start(f32[512,128]{1,0:T(8,128)S(1)} %get-tuple-element.49), channel_id=1, source_target_pairs={{0,1},{1,2},{2,3},{3,4},{4,5},{5,6},{6,7},{7,8},{8,9},{9,10},{10,1... | collective-permute-start | bytes 786440 | tf_op jit(solution)/shard_map/ppermute | solution.py:519
  65.7 3.4 %collective-permute-start.12 = (f32[512,128]{1,0:T(8,128)S(1)}, f32[512,128]{1,0:T(8,128)S(1)}, u32[]{:S(2)}, u32[]{:S(2)}) collective-permute-start(f32[512,128]{1,0:T(8,128)S(1)} %get-tuple-element.50), channel_id=1, source_target_pairs={{1,0},{2,1},{3,2},{4,3},{5,4},{6,5},{7,6},{8,7},{9,8},{10,9},{11,1... | collective-permute-start | bytes 786440 | tf_op jit(solution)/shard_map/ppermute | solution.py:519
  69.0 1.6 %shard_map.87.base = f32[1024,128]{1,0:T(8,128)S(1)} custom-call(f32[1024,128]{1,0:T(8,128)S(1)} %get-tuple-element.28.d, f32[1024,128]{1,0:T(8,128)S(1)} %get-tuple-element.29.c, f32[1088,128]{1,0:T(8,128)S(1)} %get-tuple-element.38.xo, f32[1024,128]{1,0:T(8,128)S(1)} %get-tuple-element.39.xe, f32[1280,128]{1,0:T(8,128)S(1)} %get-tuple-element.40.xy, ...), custom_call_target="tpu_custom_call" | custom-call | tf_op jit(solution)/shard_map/pallas_call | solution.py:484
  70.7 0.0 collective-permute-done.9.gb
  70.7 3.0 %collective-permute-done.11.yl = f32[512,128]{1,0:T(8,128)S(1)} collective-permute-done((f32[512,128]{1,0:T(8,128)S(1)}, f32[512,128]{1,0:T(8,128)S(1)}, u32[]{:S(2)}, u32[]{:S(2)}) %collective-permute-start.11) | collective-permute-done | bytes 262176 | tf_op jit(solution)/shard_map/ppermute | solution.py:519
  73.7 3.8 %collective-permute-done.12.yr = f32[512,128]{1,0:T(8,128)S(1)} collective-permute-done((f32[512,128]{1,0:T(8,128)S(1)}, f32[512,128]{1,0:T(8,128)S(1)}, u32[]{:S(2)}, u32[]{:S(2)}) %collective-permute-start.12) | collective-permute-done | bytes 262176 | tf_op jit(solution)/shard_map/ppermute | solution.py:519
  77.5 0.9 %shard_map.89 = f32[1024,128]{1,0:T(8,128)} custom-call(f32[32,128]{1,0:T(8,128)S(1)} %shard_map.82.av, f32[1024,128]{1,0:T(8,128)S(1)} %shard_map.87.base, f32[1024,128]{1,0:T(8,128)S(1)} %get-tuple-element.43.own, f32[2048,128]{1,0:T(8,128)S(1)} %collective-permute-done.8.ha.ga, f32[1024,128]{1,0:T(8,128)S(1)} %collective-permute-done.9.gb, ...), custom_call_target="tpu_custom_call" | custom-call | tf_op jit(solution)/shard_map/pallas_call | solution.py:484
Async XLA Ops:
  1.4 5.3 %copy-start.5 = (f32[2,2]{1,0:T(2,128)S(1)}, f32[2,2]{1,0:T(2,128)}, u32[]{:S(2)}) copy-start(f32[2,2]{1,0:T(2,128)} %adh.1) | copy-start | bytes 52
  1.4 9.8 %collective-permute-start = (f32[576,128]{1,0:T(8,128)S(1)}, f32[576,128]{1,0:T(8,128)S(1)}, u32[]{:S(2)}, u32[]{:S(2)}) collective-permute-start(f32[576,128]{1,0:T(8,128)S(1)} %get-tuple-element.30), channel_id=1, source_target_pairs={{0,1},{1,2},{2,3},{3,4},{4,5},{5,6},{6,7},{7,8},{8,9},{9,10},{10,1... | collective-permute-start | bytes 884744 | tf_op jit(solution)/shard_map/ppermute | solution.py:519
  4.5 11.6 %collective-permute-start.1 = (f32[576,128]{1,0:T(8,128)S(1)}, f32[576,128]{1,0:T(8,128)S(1)}, u32[]{:S(2)}, u32[]{:S(2)}) collective-permute-start(f32[576,128]{1,0:T(8,128)S(1)} %get-tuple-element.31), channel_id=1, source_target_pairs={{1,0},{2,1},{3,2},{4,3},{5,4},{6,5},{7,6},{8,7},{9,8},{10,9},{11,1... | collective-permute-start | bytes 884744 | tf_op jit(solution)/shard_map/ppermute | solution.py:519
  16.1 24.4 %copy-start = (bf16[80,160]{1,0:T(8,128)(2,1)S(1)}, bf16[80,160]{1,0:T(8,128)(2,1)}, u32[]{:S(2)}) copy-start(bf16[80,160]{1,0:T(8,128)(2,1)} %constant.10.clone.my) | copy-start | bytes 76804
  16.2 29.0 %collective-permute-start.4 = (f32[1152,128]{1,0:T(8,128)S(1)}, f32[1152,128]{1,0:T(8,128)S(1)}, u32[]{:S(2)}, u32[]{:S(2)}) collective-permute-start(f32[1152,128]{1,0:T(8,128)S(1)} %get-tuple-element.32), channel_id=1, source_target_pairs={{0,16},{16,0},{32,48},{48,32},{64,80},{80,64},{96,112},{112,96},{1... | collective-permute-start | bytes 1769480 | tf_op jit(solution)/shard_map/ppermute | solution.py:527
  20.0 25.3 %collective-permute-start.5 = (f32[1152,128]{1,0:T(8,128)S(1)}, f32[1152,128]{1,0:T(8,128)S(1)}, u32[]{:S(2)}, u32[]{:S(2)}) collective-permute-start(f32[1152,128]{1,0:T(8,128)S(1)} %get-tuple-element.33), channel_id=1, source_target_pairs={{16,32},{32,16},{48,64},{64,48},{80,96},{96,80},{112,128},{128,112... | collective-permute-start | bytes 1769480 | tf_op jit(solution)/shard_map/ppermute | solution.py:527
  24.6 20.6 %collective-permute-start.3 = (f32[1024,128]{1,0:T(8,128)S(1)}, f32[1024,128]{1,0:T(8,128)S(1)}, u32[]{:S(2)}, u32[]{:S(2)}) collective-permute-start(f32[1024,128]{1,0:T(8,128)S(1)} %get-tuple-element.28.d), channel_id=1, source_target_pairs={{16,32},{32,16},{48,64},{64,48},{80,96},{96,80},{112,128},{128,112... | collective-permute-start | bytes 1572872 | tf_op jit(solution)/shard_map/ppermute | solution.py:527
  26.7 18.5 %collective-permute-start.2 = (f32[1024,128]{1,0:T(8,128)S(1)}, f32[1024,128]{1,0:T(8,128)S(1)}, u32[]{:S(2)}, u32[]{:S(2)}) collective-permute-start(f32[1024,128]{1,0:T(8,128)S(1)} %get-tuple-element.28.d), channel_id=1, source_target_pairs={{0,16},{16,0},{32,48},{48,32},{64,80},{80,64},{96,112},{112,96},{1... | collective-permute-start | bytes 1572872 | tf_op jit(solution)/shard_map/ppermute | solution.py:527
  28.7 9.8 %collective-permute-start.6 = (f32[128,128]{1,0:T(8,128)S(1)}, f32[128,128]{1,0:T(8,128)S(1)}, u32[]{:S(2)}, u32[]{:S(2)}) collective-permute-start(f32[128,128]{1,0:T(8,128)S(1)} %get-tuple-element.34), channel_id=1, source_target_pairs={{0,32},{16,48},{32,64},{48,80},{64,96},{80,112},{96,128},{112,144}... | collective-permute-start | bytes 196616 | tf_op jit(solution)/shard_map/ppermute | solution.py:519
  38.4 6.8 %copy-start.1 = (bf16[256,128]{1,0:T(8,128)(2,1)S(1)}, bf16[256,128]{1,0:T(8,128)(2,1)}, u32[]{:S(2)}) copy-start(bf16[256,128]{1,0:T(8,128)(2,1)} %constant.14.clone.zot) | copy-start | bytes 196612
  38.4 6.8 %copy-start.2 = (bf16[256,128]{1,0:T(8,128)(2,1)S(1)}, bf16[256,128]{1,0:T(8,128)(2,1)}, u32[]{:S(2)}) copy-start(bf16[256,128]{1,0:T(8,128)(2,1)} %constant.13.clone.zo) | copy-start | bytes 196612
  38.4 6.9 %copy-start.3 = (bf16[256,128]{1,0:T(8,128)(2,1)S(1)}, bf16[256,128]{1,0:T(8,128)(2,1)}, u32[]{:S(2)}) copy-start(bf16[256,128]{1,0:T(8,128)(2,1)} %constant.12.clone.ze) | copy-start | bytes 196612
  38.4 6.9 %copy-start.4 = (bf16[64,128]{1,0:T(8,128)(2,1)S(1)}, bf16[64,128]{1,0:T(8,128)(2,1)}, u32[]{:S(2)}) copy-start(bf16[64,128]{1,0:T(8,128)(2,1)} %constant.11.clone.myt) | copy-start | bytes 49156
  38.5 6.8 %collective-permute-start.7 = (f32[128,128]{1,0:T(8,128)S(1)}, f32[128,128]{1,0:T(8,128)S(1)}, u32[]{:S(2)}, u32[]{:S(2)}) collective-permute-start(f32[128,128]{1,0:T(8,128)S(1)} %get-tuple-element.35), channel_id=1, source_target_pairs={{32,0},{48,16},{64,32},{80,48},{96,64},{112,80},{128,96},{144,112}... | collective-permute-start | bytes 196616 | tf_op jit(solution)/shard_map/ppermute | solution.py:519
  50.0 13.6 %collective-permute-start.8 = (f32[2048,128]{1,0:T(8,128)S(1)}, f32[2048,128]{1,0:T(8,128)S(1)}, u32[]{:S(2)}, u32[]{:S(2)}) collective-permute-start(f32[2048,128]{1,0:T(8,128)S(1)} %get-tuple-element.44), channel_id=1, source_target_pairs={{0,16},{16,0},{32,48},{48,32},{64,80},{80,64},{96,112},{112,96},{1... | collective-permute-start | bytes 3145736 | tf_op jit(solution)/shard_map/ppermute | solution.py:527
  52.0 11.7 %collective-permute-start.10 = (f32[1024,128]{1,0:T(8,128)S(1)}, f32[1024,128]{1,0:T(8,128)S(1)}, u32[]{:S(2)}, u32[]{:S(2)}) collective-permute-start(f32[1024,128]{1,0:T(8,128)S(1)} %get-tuple-element.48), channel_id=1, source_target_pairs={{16,32},{32,16},{48,64},{64,48},{80,96},{96,80},{112,128},{128,112... | collective-permute-start | bytes 1572872 | tf_op jit(solution)/shard_map/ppermute | solution.py:527
  55.7 15.0 %collective-permute-start.9 = (f32[1024,128]{1,0:T(8,128)S(1)}, f32[1024,128]{1,0:T(8,128)S(1)}, u32[]{:S(2)}, u32[]{:S(2)}) collective-permute-start(f32[1024,128]{1,0:T(8,128)S(1)} %get-tuple-element.45), channel_id=1, source_target_pairs={{16,32},{32,16},{48,64},{64,48},{80,96},{96,80},{112,128},{128,112... | collective-permute-start | bytes 1572872 | tf_op jit(solution)/shard_map/ppermute | solution.py:527
  63.8 10.0 %collective-permute-start.11 = (f32[512,128]{1,0:T(8,128)S(1)}, f32[512,128]{1,0:T(8,128)S(1)}, u32[]{:S(2)}, u32[]{:S(2)}) collective-permute-start(f32[512,128]{1,0:T(8,128)S(1)} %get-tuple-element.49), channel_id=1, source_target_pairs={{0,1},{1,2},{2,3},{3,4},{4,5},{5,6},{6,7},{7,8},{8,9},{9,10},{10,1... | collective-permute-start | bytes 786440 | tf_op jit(solution)/shard_map/ppermute | solution.py:519
  65.7 11.8 %collective-permute-start.12 = (f32[512,128]{1,0:T(8,128)S(1)}, f32[512,128]{1,0:T(8,128)S(1)}, u32[]{:S(2)}, u32[]{:S(2)}) collective-permute-start(f32[512,128]{1,0:T(8,128)S(1)} %get-tuple-element.50), channel_id=1, source_target_pairs={{1,0},{2,1},{3,2},{4,3},{5,4},{6,5},{7,6},{8,7},{9,8},{10,9},{11,1... | collective-permute-start | bytes 786440 | tf_op jit(solution)/shard_map/ppermute | solution.py:519
